TPU v7x, 256 devices: a whole 4x4x8 slice. The times are simulated.
256 devices in a mesh: tile: 64 (over z_hi, x, y, core), agent: 4 (over z_lo).
Axes of the slice: x: 4, y: 4, z: 8 (z_hi: 2, z_lo: 4; z = z_hi * 4 + z_lo), core: 2. Of those that a mesh axis runs over, the one named last changes fastest.
Arguments:
- view_tile: bfloat16 [16, 64, 768, 1024], P('agent', 'tile'), may hold values from -0.0234375 to 0.0234375
- block_mask: int32 [16, 64, 6, 8], P('agent', 'tile'), may hold values 0 or 1
- sinogram: float32 [16, 32, 768], P('agent'), may hold values from -24 to 24
- bin_weight: float32 [16, 32, 768], P('agent'), may hold values from 0.2 to 0.6
- model_state: float32 [64, 32, 1024], P('tile', 'agent'), may hold values from -6 to 6
- planar_state: float32 [64, 32, 1024], P('tile', 'agent'), may hold values from -6 to 6
- sagittal_state: float32 [64, 32, 1024], P('tile', 'agent'), may hold values from -6 to 6
- planar_in: float32 [9, 16], replicated, may hold values from -3 to 3
- planar_mid: float32 [3, 9, 16, 16], replicated, may hold values from -0.75 to 0.75
- planar_out: float32 [9, 16], replicated, may hold values from -0.5 to 0.5
- sagittal_in: float32 [9, 16], replicated, may hold values from -3 to 3
- sagittal_mid: float32 [3, 9, 16, 16], replicated, may hold values from -0.75 to 0.75
- sagittal_out: float32 [9, 16], replicated, may hold values from -0.5 to 0.5
Outputs:
- model_next: float32 [64, 32, 1024], P('tile', 'agent')
- planar_next: float32 [64, 32, 1024], P('tile', 'agent')
- sagittal_next: float32 [64, 32, 1024], P('tile', 'agent')
All inputs are finite; a program needn't handle non-finite values. No bound on the sum of `block_mask` on one device may be relied on, other than what follows from the above.
Results may differ from a plain program's by a relative error of at most 0.0055.
Values may be sent and summed in bfloat16 or wider, within the bound.
No kernel may reach another device: no remote copies, remote signals or barrier semaphores. Data moves between devices by JAX's collectives and lax.ppermute only.
A program may use at most 128 MiB of HBM per device.

v0:
```python
import jax
import jax.numpy as jnp
from jax import lax
from jax.experimental import pallas as pl
from jax.experimental.pallas import tpu as pltpu
from jax.sharding import Mesh, PartitionSpec as P


PX = 8
HALO = 5
LANES = 128
SPLIT = 2
PLANE = ("x", "y", "core")
TILE = ("zh",) + PLANE

bf16 = jnp.bfloat16
f32 = jnp.float32
VMEM = pl.BlockSpec(memory_space=pltpu.VMEM)
SMEM = pl.BlockSpec(memory_space=pltpu.SMEM)
HBM = pl.BlockSpec(memory_space=pltpu.HBM)


def params(mebibytes, axes=0):
    return pltpu.CompilerParams(
        vmem_limit_bytes=mebibytes << 20, dimension_semantics=("arbitrary",) * axes or None
    )


def onchip(value):
    return pltpu.with_memory_space_constraint(value, pltpu.VMEM)


def fetch(source, target, sems):
    views, bins, _ = target.shape
    rows = bins // SPLIT
    copies = []
    for v in range(views):
        for h in range(SPLIT):
            copy = pltpu.make_async_copy(
                source.at[v, pl.ds(h * rows, rows)],
                target.at[v, pl.ds(h * rows, rows)],
                sems.at[v * SPLIT + h],
            )
            copy.start()
            copies.append((v, h * rows, copy))
    return copies


def offchip(value):
    return pltpu.with_memory_space_constraint(value, pltpu.HBM)


def mask_blocks(view_tile, mask):
    views, _, bins, voxels = view_tile.shape
    rows = bins // SPLIT

    def kernel(mask_ref, view_ref, chip_ref, sems):
        for v, first, copy in fetch(view_ref.at[:, 0], chip_ref, sems):
            copy.wait()
            for j in range(first, first + rows, LANES):
                for k in range(voxels // LANES):
                    keep = jnp.full((16, LANES), mask_ref[v, 0, j // LANES, k].astype(f32)).astype(bf16)
                    at = (v, slice(j, j + LANES), slice(k * LANES, (k + 1) * LANES))
                    block = chip_ref[at].reshape(8, 16, LANES) * keep[None]
                    chip_ref[at] = block.reshape(LANES, LANES)

    return pl.pallas_call(
        kernel,
        out_shape=pltpu.VMEM((views, bins, voxels), bf16),
        in_specs=[SMEM, HBM],
        out_specs=VMEM,
        scratch_shapes=[pltpu.SemaphoreType.DMA((views * SPLIT,))],
        compiler_params=params(16),
        name="mask_blocks",
    )(mask, offchip(view_tile))


def project_tiles(low, matrix_ref, out_ref):
    views, bins, _ = matrix_ref.shape
    groups, blocks = low.shape[0] // 8, bins // LANES
    for v in range(views):
        result = lax.dot_general(
            low, matrix_ref[v], (((1,), (1,)), ((), ())), preferred_element_type=f32
        ).astype(bf16)
        for g in range(groups):
            for j in range(blocks):
                out_ref[(v * groups + g) * blocks + j] = result[8 * g : 8 * g + 8, j * LANES : (j + 1) * LANES]


def project_first(parts, matrix, me):
    own, voxels = parts[0].shape
    groups = len(parts)
    views, bins, _ = matrix.shape

    def kernel(me_ref, *refs):
        part_refs, (matrix_ref, out_ref, anchor_ref, main_ref, sems) = refs[:groups], refs[groups:]
        copies = fetch(matrix_ref, main_ref, sems)
        for k in range(groups):
            first = pl.multiple_of(jnp.bitwise_xor(me_ref[0], k) * own, own)
            anchor_ref[pl.ds(first, own), :] = part_refs[k][...].astype(f32)
        project_tiles(anchor_ref[...].astype(bf16), matrix_ref, out_ref)
        for *_, copy in copies:
            copy.wait()

    return pl.pallas_call(
        kernel,
        out_shape=[
            jax.ShapeDtypeStruct((views * groups * bins // LANES, own, LANES), bf16),
            jax.ShapeDtypeStruct((groups * own, voxels), f32),
            pltpu.HBM(matrix.shape, bf16),
        ],
        in_specs=[SMEM] + [VMEM] * (groups + 1),
        out_specs=[VMEM, VMEM, HBM],
        scratch_shapes=[pltpu.SemaphoreType.DMA((views * SPLIT,))],
        compiler_params=params(16),
        name="project_first",
    )(me, *[onchip(p) for p in parts], onchip(matrix))


def project_next(anchor, pieces, matrix, me):
    slices, voxels = anchor.shape
    views, bins, _ = matrix.shape
    own = 8
    count = len(pieces)

    def kernel(me_ref, anchor_ref, *refs):
        piece_refs, (matrix_ref, out_ref, own_ref, gradient_ref) = refs[:count], refs[count:]
        gradient = piece_refs[0][...]
        for ref in piece_refs[1:]:
            gradient = gradient + ref[...].astype(f32)
        gradient_ref[...] = gradient
        low = (anchor_ref[...] - 0.5 * gradient).astype(bf16)
        own_ref[...] = gradient_ref[pl.ds(pl.multiple_of(me_ref[0] * own, own), own), :]
        project_tiles(low, matrix_ref, out_ref)

    return pl.pallas_call(
        kernel,
        out_shape=[
            jax.ShapeDtypeStruct((views * slices // own * bins // LANES, own, LANES), bf16),
            jax.ShapeDtypeStruct((own, voxels), f32),
        ],
        in_specs=[SMEM] + [VMEM] * (count + 2),
        out_specs=[VMEM, VMEM],
        scratch_shapes=[pltpu.VMEM((slices, voxels), f32)],
        compiler_params=params(16),
        name="project_next",
    )(me, onchip(anchor), *[onchip(p) for p in pieces], onchip(matrix))


def back_project(misfit, matrix, me, groups, whole):
    views, bins, voxels = matrix.shape
    own = misfit.shape[1]
    blocks = bins // LANES
    rows = bins // SPLIT

    def kernel(me_ref, misfit_ref, matrix_ref, *refs):
        *outs, chip_ref, sems = refs if whole else refs[:-3] + refs[-2:]
        total = None
        for v, first, copy in fetch(matrix_ref, chip_ref, sems):
            left = jnp.concatenate(
                [
                    jnp.concatenate(
                        [
                            misfit_ref[(v * groups + g) * blocks + j].astype(f32)
                            for j in range(first // LANES, (first + rows) // LANES)
                        ],
                        axis=1,
                    )
                    for g in range(groups)
                ],
                axis=0,
            ).astype(bf16)
            copy.wait()
            part = jnp.dot(left, chip_ref[v, first : first + rows, :], preferred_element_type=f32)
            total = part if total is None else total + part
        if whole:
            outs[0][...] = total
            outs[1][...] = total.astype(bf16)
        else:
            total_ref = refs[-3]
            total_ref[...] = total
            for k in range(groups):
                first = pl.multiple_of(jnp.bitwise_xor(me_ref[0], k) * own, own)
                outs[k][...] = total_ref[pl.ds(first, own), :].astype(outs[k].dtype)

    if whole:
        outs = [jax.ShapeDtypeStruct((groups * own, voxels), t) for t in (f32, bf16)]
        outs.append(pltpu.VMEM(matrix.shape, bf16))
        scratch = []
    else:
        outs = [jax.ShapeDtypeStruct((own, voxels), f32 if k == 0 else bf16) for k in range(groups)]
        scratch = [pltpu.VMEM((groups * own, voxels), f32), pltpu.VMEM(matrix.shape, bf16)]
    return pl.pallas_call(
        kernel,
        out_shape=outs,
        in_specs=[SMEM, VMEM, HBM],
        out_specs=[VMEM] * len(outs),
        scratch_shapes=scratch + [pltpu.SemaphoreType.DMA((views * SPLIT,))],
        compiler_params=params(16),
        name="back_project",
    )(me, onchip(misfit), offchip(matrix))


def spread_misfit(half, other, sino, weight, copies):
    def kernel(half_ref, other_ref, sino_ref, weight_ref, out_ref):
        value = (weight_ref[...] * ((half_ref[...] + other_ref[...]) - sino_ref[...])).astype(bf16)
        for i in range(copies):
            out_ref[i] = value

    return pl.pallas_call(
        kernel,
        out_shape=jax.ShapeDtypeStruct((copies,) + half.shape, bf16),
        in_specs=[VMEM] * 4,
        out_specs=VMEM,
        compiler_params=params(4),
        name="spread_misfit",
    )(*[onchip(v) for v in (half, other, sino, weight)])


def halves(value):
    high = value.astype(bf16)
    return high, (value - high.astype(f32)).astype(bf16)


def product(weights, state_hi, state_lo):
    hi, lo = weights
    rows = hi.shape[0]
    both = jnp.dot(jnp.concatenate([hi, lo], axis=0), state_hi, preferred_element_type=f32)
    return both[:rows] + both[rows:] + jnp.dot(hi, state_lo, preferred_element_type=f32)


def denoise(low, own, high, first_in, middle, last_out, at, count):
    rows, width = own.shape
    depth, taps, hidden, _ = middle.shape
    step = taps * hidden // 3
    most = rows + 2 * (HALO - 1)
    tall = most + 2 + (-(most + 2)) % 8

    def kernel(at_ref, low_ref, own_ref, high_ref, first_ref, mid_ref, last_ref, out_ref, hi_ref, lo_ref):
        lane = lax.broadcasted_iota(jnp.int32, (1, LANES), 1)
        not_first = (lane != 0).astype(f32)
        not_last = (lane != LANES - 1).astype(f32)

        def shifted(value):
            left, right = [], []
            for b in range(width // LANES):
                piece = value[:, b * LANES : (b + 1) * LANES]
                left.append(pltpu.roll(piece, 1, 1) * not_first)
                right.append(pltpu.roll(piece, LANES - 1, 1) * not_last)
            return jnp.concatenate(left, axis=1), value, jnp.concatenate(right, axis=1)

        def keep(layer, row, values):
            reach = HALO - 1 - layer
            index = at_ref[0] * rows + (row - reach)
            inside = (index >= 0) & (index < count * rows)
            state = jnp.maximum(values, 0.0) * inside.astype(f32)
            for e, moved in enumerate(shifted(state)):
                at_row = step * row + hidden * e
                hi, lo = halves(moved)
                hi_ref[at_row : at_row + hidden, :] = hi
                lo_ref[at_row : at_row + hidden, :] = lo

        def banded(blocks, outs):
            blank = lambda n: [jnp.zeros((blocks[0].shape[0], n), f32)] if n else []
            return jnp.concatenate(
                [
                    jnp.concatenate(blank(step * i) + blocks + blank(step * (outs - 1 - i)), axis=1)
                    for i in range(outs)
                ],
                axis=0,
            )

        shape = (most, hidden, 3 * tall)
        out_row = lax.broadcasted_iota(jnp.int32, shape, 0)
        column = lax.broadcasted_iota(jnp.int32, shape, 2)
        spread = jnp.zeros(shape, f32)
        for tap in range(9):
            a, e = tap // 3, tap % 3
            chosen = column == out_row + (a + e * tall)
            spread = jnp.where(chosen, first_ref[:, tap : tap + 1][None], spread)
        spread = spread.reshape(most * hidden, 3 * tall)

        field = jnp.concatenate(
            [low_ref[...], own_ref[...], high_ref[...], jnp.zeros((tall - rows - 2 * HALO, width), f32)],
            axis=0,
        )
        state_hi, state_lo = halves(jnp.concatenate(shifted(field), axis=0))
        values = product(halves(spread), state_hi, state_lo)
        live = most
        for r in range(live):
            keep(0, r, values[hidden * r : hidden * (r + 1)])
        for layer in range(depth):
            weights = halves(banded([mid_ref[layer, t] for t in range(taps)], 3))
            live -= 2
            for r in range(0, live, 3):
                take = min(3, live - r)
                used = step * (take + 2)
                chunk = [w[: hidden * take, :used] for w in weights]
                state_hi = hi_ref[step * r : step * r + used, :]
                state_lo = lo_ref[step * r : step * r + used, :]
                values = product(chunk, state_hi, state_lo)
                for i in range(take):
                    keep(layer + 1, r + i, values[hidden * i : hidden * (i + 1)])
        used = step * live
        weights = halves(banded([last_ref[t : t + 1, :] for t in range(taps)], rows))
        out_ref[...] = own_ref[...] - product(weights, hi_ref[:used, :], lo_ref[:used, :])

    return pl.pallas_call(
        kernel,
        out_shape=jax.ShapeDtypeStruct((rows, width), f32),
        in_specs=[SMEM] + [VMEM] * 6,
        out_specs=VMEM,
        scratch_shapes=[pltpu.VMEM((most * step, width), bf16)] * 2,
        compiler_params=params(24),
        name="denoise",
    )(at, *[onchip(v) for v in (low, own, high, first_in, middle, last_out)])


def line(count, shift):
    return [(i, i + shift) for i in range(count) if 0 <= i + shift < count]


def from_below(field, axis, count):
    return lax.ppermute(field[-HALO:], axis, line(count, 1))


def from_above(field, axis, count):
    return lax.ppermute(field[:HALO], axis, line(count, -1))


def swap(value, agents, k):
    return lax.ppermute(value, "agent", [(i, i ^ k) for i in range(agents)])


def by_row(state):
    own, voxels = state.shape
    return state.reshape(own, PX, voxels // PX).transpose(1, 0, 2).reshape(PX, own * (voxels // PX))


def body(
    view_tile,
    block_mask,
    sinogram,
    bin_weight,
    model_state,
    planar_state,
    sagittal_state,
    planar_in,
    planar_mid,
    planar_out,
    sagittal_in,
    sagittal_mid,
    sagittal_out,
):
    agents = lax.axis_size("agent")
    tiles = lax.axis_size(TILE)
    spread = lax.axis_size(PLANE)
    spot = lax.axis_index(PLANE)
    own = model_state.shape[1]
    views, _, bins, _ = view_tile.shape
    per = views * agents * (bins // LANES) // spread
    agent = lax.axis_index("agent").reshape(1).astype(jnp.int32)
    tile_at = lax.axis_index(TILE).reshape(1).astype(jnp.int32)
    model_state, planar_state, sagittal_state = model_state[0], planar_state[0], sagittal_state[0]

    def share(values):
        tiled = values.reshape(views, agents, own, bins // LANES, LANES).transpose(0, 1, 3, 2, 4)
        return lax.dynamic_index_in_dim(tiled.reshape(spread, per, own, LANES), spot, 0, keepdims=False)

    def gathered(sent):
        got = lax.all_to_all(sent.reshape(spread, per, own, LANES), PLANE, 0, 0)
        half = got.astype(f32).sum(axis=0)
        other = lax.ppermute(half, "zh", [(0, 1), (1, 0)])
        spreaded = spread_misfit(half, other, share(sinogram), share(bin_weight), spread)
        misfit = lax.all_to_all(spreaded, PLANE, 0, 0)
        return misfit.reshape(spread * per, own, LANES)

    low = model_state.astype(bf16)
    parts = [low] + [swap(low, agents, k) for k in range(1, agents)]
    chip = mask_blocks(view_tile, block_mask)
    sent, anchor, matrix = project_first(parts, chip, agent)

    plane, plane_in, side_in, tile_at = lax.optimization_barrier(
        (by_row(planar_state), planar_in.T, sagittal_in.T, tile_at)
    )
    plane_low = from_below(plane, TILE, tiles)
    plane_high = from_above(plane, TILE, tiles)
    side_low = from_below(sagittal_state, "agent", agents)
    side_high = from_above(sagittal_state, "agent", agents)

    misfit = gathered(sent)
    total, piece, chip = back_project(misfit, matrix, agent, agents, True)
    pieces = [total] + [swap(piece, agents, k) for k in range(1, agents)]
    sent, gradient = project_next(anchor, pieces, chip, agent)
    guess = model_state - 0.5 * gradient

    misfit = gathered(sent)
    pieces = back_project(misfit, matrix, agent, agents, False)
    pieces = [pieces[0]] + [swap(pieces[k], agents, k) for k in range(1, agents)]
    gradient = sum(piece.astype(f32) for piece in pieces)
    model_image = guess - 0.5 * (gradient + (guess - model_state))

    planar_image = by_row(denoise(plane_low, plane, plane_high, plane_in, planar_mid, planar_out, tile_at, tiles))
    sagittal_image = denoise(side_low, sagittal_state, side_high, side_in, sagittal_mid, sagittal_out, agent, agents)

    reflect_model = 2.0 * model_image - model_state
    reflect_plane = 2.0 * planar_image - planar_state
    reflect_side = 2.0 * sagittal_image - sagittal_state
    consensus = 0.5 * reflect_model + 0.25 * reflect_plane + 0.25 * reflect_side
    model_next = 0.5 * model_state + 0.5 * (2.0 * consensus - reflect_model)
    planar_next = 0.5 * planar_state + 0.5 * (2.0 * consensus - reflect_plane)
    sagittal_next = 0.5 * sagittal_state + 0.5 * (2.0 * consensus - reflect_side)
    return (model_next[None], planar_next[None], sagittal_next[None])


def solution(mesh):
    fine = Mesh(mesh.devices.reshape(2, 4, 4, 2, 4), TILE + ("agent",))
    return jax.shard_map(
        body,
        mesh=fine,
        in_specs=(
            P("agent", TILE, None, None),
            P("agent", TILE, None, None),
            P("agent", None, None),
            P("agent", None, None),
            P(TILE, "agent", None),
            P(TILE, "agent", None),
            P(TILE, "agent", None),
            P(),
            P(),
            P(),
            P(),
            P(),
            P(),
        ),
        out_specs=(P(TILE, "agent", None),) * 3,
        check_vma=False,
    )
```

profile of v0, /device:TPU:2, one launch (start us, length us, event | category | flops | bytes accessed | tf_op | source)
XLA Modules:
  0.0 116.7 jit_solution(10469377540246674560)
XLA Ops:
  0.6 0.8 bitcast_convert_fusion.refs_0_
  1.4 1.9 %collective-permute-start = (bf16[8,1024]{1,0:T(8,128)(2,1)S(1)}, bf16[8,1024]{1,0:T(8,128)(2,1)S(1)}, u32[]{:S(2)}, u32[]{:S(2)}) collective-permute-start(bf16[8,1024]{1,0:T(8,128)(2,1)S(1)} %bitcast_convert_fusion.refs_0_), channel_id=1, source_target_pairs={{0,1},{1,0},{2,3},{3,2},{4,5},{5,4},{6,7},{7,6},{8,9},{9,8},{10,11... | collective-permute-start | bytes 49160 | tf_op jit(solution)/shard_map/ppermute | solution.py:332
  3.3 3.3 %collective-permute-start.1 = (bf16[8,1024]{1,0:T(8,128)(2,1)S(1)}, bf16[8,1024]{1,0:T(8,128)(2,1)S(1)}, u32[]{:S(2)}, u32[]{:S(2)}) collective-permute-start(bf16[8,1024]{1,0:T(8,128)(2,1)S(1)} %bitcast_convert_fusion.refs_0_), channel_id=1, source_target_pairs={{0,2},{1,3},{2,0},{3,1},{4,6},{5,7},{6,4},{7,5},{8,10},{9,11},{10,... | collective-permute-start | bytes 49160 | tf_op jit(solution)/shard_map/ppermute | solution.py:332
  6.6 0.0 collective-permute-start.2
  6.6 0.7 copy.16.mask_ref
  7.3 3.8 %mask_blocks.1.refs_4_ = bf16[4,768,1024]{2,1,0:T(8,128)(2,1)S(1)} custom-call(s32[4,1,6,8]{3,2,1,0:T(8,128)S(1)} %copy.16.mask_ref, bf16[4,1,768,1024]{3,2,1,0:T(8,128)(2,1)} %view_ref.1), custom_call_target="tpu_custom_call" | custom-call | tf_op jit(solution)/shard_map/mask_blocks/pallas_call | solution.py:67
  11.1 0.0 collective-permute-done.refs_1_
  11.2 0.0 collective-permute-done.1.refs_2_
  11.2 1.0 collective-permute-done.2.refs_3_
  12.1 3.4 %project_first.1 = (bf16[96,8,128]{2,1,0:T(8,128)(2,1)}, f32[32,1024]{1,0:T(8,128)S(1)}, bf16[4,768,1024]{2,1,0:T(8,128)(2,1)}) custom-call(s32[1]{0:T(128)} %bitcast.1.me_ref.at_ref, bf16[8,1024]{1,0:T(8,128)(2,1)S(1)} %bitcast_convert_fusion.refs_0_, bf16[8,1024]{1,0:T(8,128)(2,1)S(1)} %collective-permute-done.refs_1_, ...), custom_call_target="tpu_custom_call" | custom-call | tf_op jit(solution)/shard_map/project_first/pallas_call | solution.py:105
  15.5 7.6 %all-to-all-start = ((bf16[32,3,8,128]{3,2,1,0:T(8,128)(2,1)}), bf16[32,3,8,128]{3,2,1,0:T(8,128)(2,1)S(1)}, u32[]{:S(2)}, u32[]{:S(2)}) async-start(bf16[32,3,8,128]{3,2,1,0:T(8,128)(2,1)} %bitcast.2), calls=%async_computation | async-start | bytes 393216 | tf_op jit(solution)/shard_map/all_to_all | solution.py:371
  23.2 7.1 %all-to-all-done = bf16[32,3,8,128]{3,2,1,0:T(8,128)(2,1)S(1)} async-done(((bf16[32,3,8,128]{3,2,1,0:T(8,128)(2,1)}), bf16[32,3,8,128]{3,2,1,0:T(8,128)(2,1)S(1)}, u32[]{:S(2)}, u32[]{:S(2)}) %all-to-all-start) | async-done | bytes 196640 | tf_op jit(solution)/shard_map/all_to_all | solution.py:371
  30.3 5.5 %collective-permute-start.3 = (f32[3,8,128]{2,1,0:T(8,128)S(1)}, f32[3,8,128]{2,1,0:T(8,128)S(1)}, u32[]{:S(2)}, u32[]{:S(2)}) collective-permute-start(f32[3,8,128]{2,1,0:T(8,128)S(1)} %convert_reduce_fusion.1.half_ref), channel_id=1, source_target_pairs={{0,128},{128,0},{1,129},{129,1},{2,130},{130,2},{3,131},{131,3},{4... | collective-permute-start | bytes 36872 | tf_op jit(solution)/shard_map/ppermute | solution.py:373
  35.9 0.7 dynamic-slice_bitcast_fusion
  36.6 1.4 %collective-permute-done.3.other_ref = f32[3,8,128]{2,1,0:T(8,128)S(1)} collective-permute-done((f32[3,8,128]{2,1,0:T(8,128)S(1)}, f32[3,8,128]{2,1,0:T(8,128)S(1)}, u32[]{:S(2)}, u32[]{:S(2)}) %collective-permute-start.3) | collective-permute-done | bytes 12320 | tf_op jit(solution)/shard_map/ppermute | solution.py:373
  38.1 11.8 %all_to_all.20 = bf16[32,3,8,128]{3,2,1,0:T(8,128)(2,1)S(1)} all-to-all(bf16[32,3,8,128]{3,2,1,0:T(8,128)(2,1)S(1)} %spread_misfit.2), channel_id=1, replica_groups=mesh['zh'=2,'x'=4,'y'=4,'core'=2,'agent'=4] {'x','y','core'}, dimensions={0} | all-to-all | bytes 393216 | tf_op jit(solution)/shard_map/all_to_all | solution.py:375
  49.9 0.0 copy-start.5
  49.9 0.0 copy-start.1
  49.9 0.0 copy-start.3
  49.9 3.2 %back_project.2 = (f32[32,1024]{1,0:T(8,128)S(1)}, bf16[32,1024]{1,0:T(8,128)(2,1)S(1)}, bf16[4,768,1024]{2,1,0:T(8,128)(2,1)S(1)}) custom-call(s32[1]{0:T(128)} %bitcast.1.me_ref.at_ref, bf16[96,8,128]{2,1,0:T(8,128)(2,1)S(1)} %bitcast.90, bf16[4,768,1024]{2,1,0:T(8,128)(2,1)} %get-tuple-element.21.matrix_ref), custom_call_target="tpu_custom_call" | custom-call | tf_op jit(solution)/shard_map/back_project/pallas_call | solution.py:193
  53.1 0.1 collective-permute-start.4
  53.2 3.4 %collective-permute-start.5 = (bf16[32,1024]{1,0:T(8,128)(2,1)S(1)}, bf16[32,1024]{1,0:T(8,128)(2,1)S(1)}, u32[]{:S(2)}, u32[]{:S(2)}) collective-permute-start(bf16[32,1024]{1,0:T(8,128)(2,1)S(1)} %get-tuple-element.23), channel_id=1, source_target_pairs={{0,2},{1,3},{2,0},{3,1},{4,6},{5,7},{6,4},{7,5},{8,10},{9,11},{10,... | collective-permute-start | bytes 196616 | tf_op jit(solution)/shard_map/ppermute | solution.py:332
  56.7 0.9 collective-permute-start.6
  57.6 0.0 collective-permute-done.4.refs_1_
  57.6 3.1 %collective-permute-done.5.refs_2_ = bf16[32,1024]{1,0:T(8,128)(2,1)S(1)} collective-permute-done((bf16[32,1024]{1,0:T(8,128)(2,1)S(1)}, bf16[32,1024]{1,0:T(8,128)(2,1)S(1)}, u32[]{:S(2)}, u32[]{:S(2)}) %collective-permute-start.5) | collective-permute-done | bytes 65568 | tf_op jit(solution)/shard_map/ppermute | solution.py:332
  60.7 2.1 %collective-permute-done.6.refs_3_ = bf16[32,1024]{1,0:T(8,128)(2,1)S(1)} collective-permute-done((bf16[32,1024]{1,0:T(8,128)(2,1)S(1)}, bf16[32,1024]{1,0:T(8,128)(2,1)S(1)}, u32[]{:S(2)}, u32[]{:S(2)}) %collective-permute-start.6) | collective-permute-done | bytes 65568 | tf_op jit(solution)/shard_map/ppermute | solution.py:332
  62.8 2.6 %project_next.1 = (bf16[96,8,128]{2,1,0:T(8,128)(2,1)}, f32[8,1024]{1,0:T(8,128)S(1)}) custom-call(s32[1]{0:T(128)} %bitcast.1.me_ref.at_ref, f32[32,1024]{1,0:T(8,128)S(1)} %get-tuple-element.19.anchor_ref, f32[32,1024]{1,0:T(8,128)S(1)} %get-tuple-element.22.refs_0_, bf16[32,1024]{1,0:T(8,128)(2,1)S(1)} %collective-permute-done.4.refs_1_, ...), custom_call_target="tpu_custom_call" | custom-call | tf_op jit(solution)/shard_map/project_next/pallas_call | solution.py:136
  65.5 5.0 %all-to-all-start.2 = ((bf16[32,3,8,128]{3,2,1,0:T(8,128)(2,1)}), bf16[32,3,8,128]{3,2,1,0:T(8,128)(2,1)S(1)}, u32[]{:S(2)}, u32[]{:S(2)}) async-start(bf16[32,3,8,128]{3,2,1,0:T(8,128)(2,1)} %bitcast.12), calls=%async_computation.2 | async-start | bytes 393216 | tf_op jit(solution)/shard_map/all_to_all | solution.py:371
  70.5 0.0 copy-done.5
  70.5 0.0 copy-done.7
  70.5 0.1 copy.18
  70.6 0.0 copy-done.8
  70.6 0.1 copy.19
  70.7 7.0 %all-to-all-done.2 = bf16[32,3,8,128]{3,2,1,0:T(8,128)(2,1)S(1)} async-done(((bf16[32,3,8,128]{3,2,1,0:T(8,128)(2,1)}), bf16[32,3,8,128]{3,2,1,0:T(8,128)(2,1)S(1)}, u32[]{:S(2)}, u32[]{:S(2)}) %all-to-all-start.2) | async-done | bytes 196640 | tf_op jit(solution)/shard_map/all_to_all | solution.py:371
  77.7 4.7 %collective-permute-start.7 = (f32[3,8,128]{2,1,0:T(8,128)S(1)}, f32[3,8,128]{2,1,0:T(8,128)S(1)}, u32[]{:S(2)}, u32[]{:S(2)}) collective-permute-start(f32[3,8,128]{2,1,0:T(8,128)S(1)} %convert_reduce_fusion.half_ref), channel_id=1, source_target_pairs={{0,128},{128,0},{1,129},{129,1},{2,130},{130,2},{3,131},{131,3},{4... | collective-permute-start | bytes 36872 | tf_op jit(solution)/shard_map/ppermute | solution.py:373
  82.5 1.9 %collective-permute-start.11 = (f32[5,1024]{1,0:T(8,128)S(1)}, f32[5,1024]{1,0:T(8,128)S(1)}, u32[]{:S(2)}, u32[]{:S(2)}) collective-permute-start(f32[5,1024]{1,0:T(8,128)S(1)} %get-tuple-element.41), channel_id=1, source_target_pairs={{0,4},{4,8},{8,12},{12,16},{16,20},{20,24},{24,28},{28,32},{32,36}... | collective-permute-start | bytes 61448 | tf_op jit(solution)/shard_map/ppermute | solution.py:324
  84.4 5.8 %collective-permute-start.12 = (f32[5,1024]{1,0:T(8,128)S(1)}, f32[5,1024]{1,0:T(8,128)S(1)}, u32[]{:S(2)}, u32[]{:S(2)}) collective-permute-start(f32[5,1024]{1,0:T(8,128)S(1)} %get-tuple-element.40), channel_id=1, source_target_pairs={{4,0},{8,4},{12,8},{16,12},{20,16},{24,20},{28,24},{32,28},{36,32}... | collective-permute-start | bytes 61448 | tf_op jit(solution)/shard_map/ppermute | solution.py:328
  90.1 0.0 collective-permute-done.7.other_ref
  90.1 0.7 spread_misfit.3
  90.8 4.9 %all-to-all-start.3 = ((bf16[32,3,8,128]{3,2,1,0:T(8,128)(2,1)}), bf16[32,3,8,128]{3,2,1,0:T(8,128)(2,1)S(1)}, u32[]{:S(2)}, u32[]{:S(2)}) async-start(bf16[32,3,8,128]{3,2,1,0:T(8,128)(2,1)} %spread_misfit.3), calls=%async_computation.3 | async-start | bytes 393216 | tf_op jit(solution)/shard_map/all_to_all | solution.py:375
  95.7 0.0 copy-done
  95.7 2.7 %collective-permute-start.13 = (f32[5,1024]{1,0:T(8,128)S(1)}, f32[5,1024]{1,0:T(8,128)S(1)}, u32[]{:S(2)}, u32[]{:S(2)}) collective-permute-start(f32[5,1024]{1,0:T(8,128)S(1)} %get-tuple-element.43), channel_id=1, source_target_pairs={{0,1},{1,2},{2,3},{4,5},{5,6},{6,7},{8,9},{9,10},{10,11},{12,13},{... | collective-permute-start | bytes 61448 | tf_op jit(solution)/shard_map/ppermute | solution.py:324
  98.5 1.5 %collective-permute-start.14 = (f32[5,1024]{1,0:T(8,128)S(1)}, f32[5,1024]{1,0:T(8,128)S(1)}, u32[]{:S(2)}, u32[]{:S(2)}) collective-permute-start(f32[5,1024]{1,0:T(8,128)S(1)} %get-tuple-element.42), channel_id=1, source_target_pairs={{1,0},{2,1},{3,2},{5,4},{6,5},{7,6},{9,8},{10,9},{11,10},{13,12},{... | collective-permute-start | bytes 61448 | tf_op jit(solution)/shard_map/ppermute | solution.py:328
  100.0 0.0 collective-permute-done.11.low_ref
  100.0 0.0 collective-permute-done.12.high_ref
  100.0 0.0 copy-done.1
  100.0 0.0 copy-done.3
  100.0 3.3 %denoise.2 = f32[8,1024]{1,0:T(8,128)S(1)} custom-call(s32[1]{0:T(128)} %bitcast.19.at_ref, f32[5,1024]{1,0:T(8,128)S(1)} %collective-permute-done.11.low_ref, f32[8,1024]{1,0:T(8,128)S(1)} %bitcast.93, f32[5,1024]{1,0:T(8,128)S(1)} %collective-permute-done.12.high_ref, f32[16,9]{1,0:T(8,128)S(1)} %bitcast.95, f32[3,9,16,16]{3,2,1,0:T(8,128)S(1)} %copy-done.1, ...), custom_call_target="tpu_custom_call" | custom-call | tf_op jit(solution)/shard_map/denoise/pallas_call | solution.py:308
  103.3 0.0 all-to-all-done.3
  103.3 3.1 %back_project.3 = (f32[8,1024]{1,0:T(8,128)S(1)}, bf16[8,1024]{1,0:T(8,128)(2,1)S(1)}, bf16[8,1024]{1,0:T(8,128)(2,1)S(1)}, bf16[8,1024]{1,0:T(8,128)(2,1)S(1)}) custom-call(s32[1]{0:T(128)} %bitcast.1.me_ref.at_ref, bf16[96,8,128]{2,1,0:T(8,128)(2,1)S(1)} %bitcast.89, bf16[4,768,1024]{2,1,0:T(8,128)(2,1)} %get-tuple-element.21.matrix_ref), custom_call_target="tpu_custom_call" | custom-call | tf_op jit(solution)/shard_map/back_project/pallas_call | solution.py:193
  106.4 3.9 %collective-permute-start.10 = (bf16[8,1024]{1,0:T(8,128)(2,1)S(1)}, bf16[8,1024]{1,0:T(8,128)(2,1)S(1)}, u32[]{:S(2)}, u32[]{:S(2)}) collective-permute-start(bf16[8,1024]{1,0:T(8,128)(2,1)S(1)} %get-tuple-element.30), channel_id=1, source_target_pairs={{0,3},{1,2},{2,1},{3,0},{4,7},{5,6},{6,5},{7,4},{8,11},{9,10},{10,... | collective-permute-start | bytes 49160 | tf_op jit(solution)/shard_map/ppermute | solution.py:332
  110.4 0.4 collective-permute-start.8
  110.7 0.3 collective-permute-start.9
  111.0 0.0 collective-permute-done.13.low_ref
  111.0 0.0 collective-permute-done.14.high_ref
  111.0 0.0 copy-done.2
  111.0 0.0 copy-done.4
  111.1 3.3 %denoise.3 = f32[8,1024]{1,0:T(8,128)S(1)} custom-call(s32[1]{0:T(128)} %bitcast.1.me_ref.at_ref, f32[5,1024]{1,0:T(8,128)S(1)} %collective-permute-done.13.low_ref, f32[8,1024]{1,0:T(8,128)S(1)} %bitcast.91, f32[5,1024]{1,0:T(8,128)S(1)} %collective-permute-done.14.high_ref, f32[16,9]{1,0:T(8,128)S(1)} %bitcast.94, f32[3,9,16,16]{3,2,1,0:T(8,128)S(1)} %copy-done.2, ...), custom_call_target="tpu_custom_call" | custom-call | tf_op jit(solution)/shard_map/denoise/pallas_call | solution.py:308
  114.4 0.0 collective-permute-done.10
  114.4 0.0 collective-permute-done.8
  114.4 1.0 collective-permute-done.9
  115.4 0.0 copy-done.6
  115.4 0.7 multiply_bitcast_fusion
  116.0 0.6 fusion.1
  (13 shorter events, 0.1 us)
Async XLA Ops:
  1.4 9.8 %collective-permute-start = (bf16[8,1024]{1,0:T(8,128)(2,1)S(1)}, bf16[8,1024]{1,0:T(8,128)(2,1)S(1)}, u32[]{:S(2)}, u32[]{:S(2)}) collective-permute-start(bf16[8,1024]{1,0:T(8,128)(2,1)S(1)} %bitcast_convert_fusion.refs_0_), channel_id=1, source_target_pairs={{0,1},{1,0},{2,3},{3,2},{4,5},{5,4},{6,7},{7,6},{8,9},{9,8},{10,11... | collective-permute-start | bytes 49160 | tf_op jit(solution)/shard_map/ppermute | solution.py:332
  3.3 7.8 %collective-permute-start.1 = (bf16[8,1024]{1,0:T(8,128)(2,1)S(1)}, bf16[8,1024]{1,0:T(8,128)(2,1)S(1)}, u32[]{:S(2)}, u32[]{:S(2)}) collective-permute-start(bf16[8,1024]{1,0:T(8,128)(2,1)S(1)} %bitcast_convert_fusion.refs_0_), channel_id=1, source_target_pairs={{0,2},{1,3},{2,0},{3,1},{4,6},{5,7},{6,4},{7,5},{8,10},{9,11},{10,... | collective-permute-start | bytes 49160 | tf_op jit(solution)/shard_map/ppermute | solution.py:332
  6.6 5.5 %collective-permute-start.2 = (bf16[8,1024]{1,0:T(8,128)(2,1)S(1)}, bf16[8,1024]{1,0:T(8,128)(2,1)S(1)}, u32[]{:S(2)}, u32[]{:S(2)}) collective-permute-start(bf16[8,1024]{1,0:T(8,128)(2,1)S(1)} %bitcast_convert_fusion.refs_0_), channel_id=1, source_target_pairs={{0,3},{1,2},{2,1},{3,0},{4,7},{5,6},{6,5},{7,4},{8,11},{9,10},{10,... | collective-permute-start | bytes 49160 | tf_op jit(solution)/shard_map/ppermute | solution.py:332
  15.5 14.8 %all-to-all-start = ((bf16[32,3,8,128]{3,2,1,0:T(8,128)(2,1)}), bf16[32,3,8,128]{3,2,1,0:T(8,128)(2,1)S(1)}, u32[]{:S(2)}, u32[]{:S(2)}) async-start(bf16[32,3,8,128]{3,2,1,0:T(8,128)(2,1)} %bitcast.2), calls=%async_computation | async-start | bytes 393216 | tf_op jit(solution)/shard_map/all_to_all | solution.py:371
  30.3 7.7 %collective-permute-start.3 = (f32[3,8,128]{2,1,0:T(8,128)S(1)}, f32[3,8,128]{2,1,0:T(8,128)S(1)}, u32[]{:S(2)}, u32[]{:S(2)}) collective-permute-start(f32[3,8,128]{2,1,0:T(8,128)S(1)} %convert_reduce_fusion.1.half_ref), channel_id=1, source_target_pairs={{0,128},{128,0},{1,129},{129,1},{2,130},{130,2},{3,131},{131,3},{4... | collective-permute-start | bytes 36872 | tf_op jit(solution)/shard_map/ppermute | solution.py:373
  49.9 20.6 %copy-start.5 = (f32[1,8,1024]{2,1,0:T(8,128)S(1)}, f32[1,8,1024]{2,1,0:T(8,128)}, u32[]{:S(2)}) copy-start(f32[1,8,1024]{2,1,0:T(8,128)} %param.18) | copy-start | bytes 98308
  49.9 20.6 %copy-start.7 = (f32[9,16]{1,0:T(8,128)S(1)}, f32[9,16]{1,0:T(8,128)}, u32[]{:S(2)}) copy-start(f32[9,16]{1,0:T(8,128)} %param.20) | copy-start | bytes 1732
  49.9 20.7 %copy-start.8 = (f32[9,16]{1,0:T(8,128)S(1)}, f32[9,16]{1,0:T(8,128)}, u32[]{:S(2)}) copy-start(f32[9,16]{1,0:T(8,128)} %param.23) | copy-start | bytes 1732
  49.9 45.8 %copy-start = (f32[1,8,1024]{2,1,0:T(8,128)S(1)}, f32[1,8,1024]{2,1,0:T(8,128)}, u32[]{:S(2)}) copy-start(f32[1,8,1024]{2,1,0:T(8,128)} %param.19) | copy-start | bytes 98308
  49.9 50.1 %copy-start.1 = (f32[3,9,16,16]{3,2,1,0:T(8,128)S(1)}, f32[3,9,16,16]{3,2,1,0:T(8,128)}, u32[]{:S(2)}) copy-start(f32[3,9,16,16]{3,2,1,0:T(8,128)} %mid_ref.2) | copy-start | bytes 82948
  49.9 50.1 %copy-start.3 = (f32[9,16]{1,0:T(8,128)S(1)}, f32[9,16]{1,0:T(8,128)}, u32[]{:S(2)}) copy-start(f32[9,16]{1,0:T(8,128)} %last_ref.2) | copy-start | bytes 1732
  53.1 4.5 %collective-permute-start.4 = (bf16[32,1024]{1,0:T(8,128)(2,1)S(1)}, bf16[32,1024]{1,0:T(8,128)(2,1)S(1)}, u32[]{:S(2)}, u32[]{:S(2)}) collective-permute-start(bf16[32,1024]{1,0:T(8,128)(2,1)S(1)} %get-tuple-element.23), channel_id=1, source_target_pairs={{0,1},{1,0},{2,3},{3,2},{4,5},{5,4},{6,7},{7,6},{8,9},{9,8},{10,11... | collective-permute-start | bytes 196616 | tf_op jit(solution)/shard_map/ppermute | solution.py:332
  53.2 7.5 %collective-permute-start.5 = (bf16[32,1024]{1,0:T(8,128)(2,1)S(1)}, bf16[32,1024]{1,0:T(8,128)(2,1)S(1)}, u32[]{:S(2)}, u32[]{:S(2)}) collective-permute-start(bf16[32,1024]{1,0:T(8,128)(2,1)S(1)} %get-tuple-element.23), channel_id=1, source_target_pairs={{0,2},{1,3},{2,0},{3,1},{4,6},{5,7},{6,4},{7,5},{8,10},{9,11},{10,... | collective-permute-start | bytes 196616 | tf_op jit(solution)/shard_map/ppermute | solution.py:332
  56.7 6.2 %collective-permute-start.6 = (bf16[32,1024]{1,0:T(8,128)(2,1)S(1)}, bf16[32,1024]{1,0:T(8,128)(2,1)S(1)}, u32[]{:S(2)}, u32[]{:S(2)}) collective-permute-start(bf16[32,1024]{1,0:T(8,128)(2,1)S(1)} %get-tuple-element.23), channel_id=1, source_target_pairs={{0,3},{1,2},{2,1},{3,0},{4,7},{5,6},{6,5},{7,4},{8,11},{9,10},{10,... | collective-permute-start | bytes 196616 | tf_op jit(solution)/shard_map/ppermute | solution.py:332
  62.8 48.2 %copy-start.2 = (f32[3,9,16,16]{3,2,1,0:T(8,128)S(1)}, f32[3,9,16,16]{3,2,1,0:T(8,128)}, u32[]{:S(2)}) copy-start(f32[3,9,16,16]{3,2,1,0:T(8,128)} %mid_ref.3) | copy-start | bytes 82948
  62.8 48.2 %copy-start.4 = (f32[9,16]{1,0:T(8,128)S(1)}, f32[9,16]{1,0:T(8,128)}, u32[]{:S(2)}) copy-start(f32[9,16]{1,0:T(8,128)} %last_ref.3) | copy-start | bytes 1732
  62.8 52.5 %copy-start.6 = (f32[1,8,1024]{2,1,0:T(8,128)S(1)}, f32[1,8,1024]{2,1,0:T(8,128)}, u32[]{:S(2)}) copy-start(f32[1,8,1024]{2,1,0:T(8,128)} %param.17) | copy-start | bytes 98308
  65.5 12.2 %all-to-all-start.2 = ((bf16[32,3,8,128]{3,2,1,0:T(8,128)(2,1)}), bf16[32,3,8,128]{3,2,1,0:T(8,128)(2,1)S(1)}, u32[]{:S(2)}, u32[]{:S(2)}) async-start(bf16[32,3,8,128]{3,2,1,0:T(8,128)(2,1)} %bitcast.12), calls=%async_computation.2 | async-start | bytes 393216 | tf_op jit(solution)/shard_map/all_to_all | solution.py:371
  77.7 12.4 %collective-permute-start.7 = (f32[3,8,128]{2,1,0:T(8,128)S(1)}, f32[3,8,128]{2,1,0:T(8,128)S(1)}, u32[]{:S(2)}, u32[]{:S(2)}) collective-permute-start(f32[3,8,128]{2,1,0:T(8,128)S(1)} %convert_reduce_fusion.half_ref), channel_id=1, source_target_pairs={{0,128},{128,0},{1,129},{129,1},{2,130},{130,2},{3,131},{131,3},{4... | collective-permute-start | bytes 36872 | tf_op jit(solution)/shard_map/ppermute | solution.py:373
  82.5 17.5 %collective-permute-start.11 = (f32[5,1024]{1,0:T(8,128)S(1)}, f32[5,1024]{1,0:T(8,128)S(1)}, u32[]{:S(2)}, u32[]{:S(2)}) collective-permute-start(f32[5,1024]{1,0:T(8,128)S(1)} %get-tuple-element.41), channel_id=1, source_target_pairs={{0,4},{4,8},{8,12},{12,16},{16,20},{20,24},{24,28},{28,32},{32,36}... | collective-permute-start | bytes 61448 | tf_op jit(solution)/shard_map/ppermute | solution.py:324
  84.4 15.6 %collective-permute-start.12 = (f32[5,1024]{1,0:T(8,128)S(1)}, f32[5,1024]{1,0:T(8,128)S(1)}, u32[]{:S(2)}, u32[]{:S(2)}) collective-permute-start(f32[5,1024]{1,0:T(8,128)S(1)} %get-tuple-element.40), channel_id=1, source_target_pairs={{4,0},{8,4},{12,8},{16,12},{20,16},{24,20},{28,24},{32,28},{36,32}... | collective-permute-start | bytes 61448 | tf_op jit(solution)/shard_map/ppermute | solution.py:328
  90.8 12.5 %all-to-all-start.3 = ((bf16[32,3,8,128]{3,2,1,0:T(8,128)(2,1)}), bf16[32,3,8,128]{3,2,1,0:T(8,128)(2,1)S(1)}, u32[]{:S(2)}, u32[]{:S(2)}) async-start(bf16[32,3,8,128]{3,2,1,0:T(8,128)(2,1)} %spread_misfit.3), calls=%async_computation.3 | async-start | bytes 393216 | tf_op jit(solution)/shard_map/all_to_all | solution.py:375
  95.7 15.3 %collective-permute-start.13 = (f32[5,1024]{1,0:T(8,128)S(1)}, f32[5,1024]{1,0:T(8,128)S(1)}, u32[]{:S(2)}, u32[]{:S(2)}) collective-permute-start(f32[5,1024]{1,0:T(8,128)S(1)} %get-tuple-element.43), channel_id=1, source_target_pairs={{0,1},{1,2},{2,3},{4,5},{5,6},{6,7},{8,9},{9,10},{10,11},{12,13},{... | collective-permute-start | bytes 61448 | tf_op jit(solution)/shard_map/ppermute | solution.py:324
  98.5 12.6 %collective-permute-start.14 = (f32[5,1024]{1,0:T(8,128)S(1)}, f32[5,1024]{1,0:T(8,128)S(1)}, u32[]{:S(2)}, u32[]{:S(2)}) collective-permute-start(f32[5,1024]{1,0:T(8,128)S(1)} %get-tuple-element.42), channel_id=1, source_target_pairs={{1,0},{2,1},{3,2},{5,4},{6,5},{7,6},{9,8},{10,9},{11,10},{13,12},{... | collective-permute-start | bytes 61448 | tf_op jit(solution)/shard_map/ppermute | solution.py:328
  106.4 7.9 %collective-permute-start.10 = (bf16[8,1024]{1,0:T(8,128)(2,1)S(1)}, bf16[8,1024]{1,0:T(8,128)(2,1)S(1)}, u32[]{:S(2)}, u32[]{:S(2)}) collective-permute-start(bf16[8,1024]{1,0:T(8,128)(2,1)S(1)} %get-tuple-element.30), channel_id=1, source_target_pairs={{0,3},{1,2},{2,1},{3,0},{4,7},{5,6},{6,5},{7,4},{8,11},{9,10},{10,... | collective-permute-start | bytes 49160 | tf_op jit(solution)/shard_map/ppermute | solution.py:332
  110.4 4.0 %collective-permute-start.8 = (bf16[8,1024]{1,0:T(8,128)(2,1)S(1)}, bf16[8,1024]{1,0:T(8,128)(2,1)S(1)}, u32[]{:S(2)}, u32[]{:S(2)}) collective-permute-start(bf16[8,1024]{1,0:T(8,128)(2,1)S(1)} %get-tuple-element.28), channel_id=1, source_target_pairs={{0,1},{1,0},{2,3},{3,2},{4,5},{5,4},{6,7},{7,6},{8,9},{9,8},{10,11... | collective-permute-start | bytes 49160 | tf_op jit(solution)/shard_map/ppermute | solution.py:332
  110.7 4.6 %collective-permute-start.9 = (bf16[8,1024]{1,0:T(8,128)(2,1)S(1)}, bf16[8,1024]{1,0:T(8,128)(2,1)S(1)}, u32[]{:S(2)}, u32[]{:S(2)}) collective-permute-start(bf16[8,1024]{1,0:T(8,128)(2,1)S(1)} %get-tuple-element.29), channel_id=1, source_target_pairs={{0,2},{1,3},{2,0},{3,1},{4,6},{5,7},{6,4},{7,5},{8,10},{9,11},{10,... | collective-permute-start | bytes 49160 | tf_op jit(solution)/shard_map/ppermute | solution.py:332
where the time goes:
time: 119 us; the launch traced here: 117 us
  starting transfers between devices  53.9 us (45%)
  Pallas kernels  23.5 us (20%)
  waiting for transfers between devices  22.7 us (19%)
  blocking collectives  11.8 us (10%)
  other arithmetic  2.15 us (2%)
  local copies, waits for them, and re-layouts  1.66 us (1%)
    ppermute x9, starting transfers between devices, swap(): return lax.ppermute(value, 'agent', [(i, i ^ k) for i in range(agents)])  14.2 us
    all_to_all x2, waiting for transfers between devices, gathered(): got = lax.all_to_all(sent.reshape(spread, per, own, LANES), PLANE, 0, 0)  14.1 us
    all_to_all x2, starting transfers between devices, gathered(): got = lax.all_to_all(sent.reshape(spread, per, own, LANES), PLANE, 0, 0)  12.7 us
    all_to_all x1, blocking collectives, gathered(): misfit = lax.all_to_all(spreaded, PLANE, 0, 0)  11.8 us
    ppermute x2, starting transfers between devices, gathered(): other = lax.ppermute(half, 'zh', [(0, 1), (1, 0)])  10.2 us
    ppermute x2, starting transfers between devices, from_above(): return lax.ppermute(field[:HALO], axis, line(count, -1))  7.22 us
    ppermute x9, waiting for transfers between devices, swap(): return lax.ppermute(value, 'agent', [(i, i ^ k) for i in range(agents)])  7.17 us
    pallas_call x2, Pallas kernels, denoise(): pl.pallas_call(kernel, out_shape=jax.ShapeDtypeStruct((rows, width), f32)...  6.59 us
  transfers between devices with their start and end apart: 18, of which 7 were waited for; matrix products, arithmetic and copies ran while one was open for 1% of the time, Pallas kernels for 12%

commit v1 on v0

--- a/solution.py
+++ b/solution.py
@@ -229,8 +229,8 @@
     return both[:rows] + both[rows:] + jnp.dot(hi, state_lo, preferred_element_type=f32)
 
 
-def denoise(low, own, high, first_in, middle, last_out, at, count):
-    rows, width = own.shape
+def denoise(low, own, high, first_in, middle, last_out, at, count, across):
+    rows, width = PX, own.shape[1]
     depth, taps, hidden, _ = middle.shape
     step = taps * hidden // 3
     most = rows + 2 * (HALO - 1)
@@ -270,6 +270,25 @@
                 axis=0,
             )
 
+        def turned(tiles):
+            turn = jnp.swapaxes(jnp.stack(tiles), 0, 1)
+            return jnp.concatenate([turn[b] for b in range(turn.shape[0])], axis=1)
+
+        def cut(value):
+            return [value[:, i : i + LANES] for i in range(0, value.shape[1], LANES)]
+
+        spare = tall - rows - 2 * HALO
+        if across:
+            tiles = cut(low_ref[...]) + cut(own_ref[...]) + cut(high_ref[...])
+            field = turned(tiles + [jnp.zeros_like(tiles[0])] * spare)
+        else:
+            field = jnp.concatenate(
+                [low_ref[...], own_ref[...], high_ref[...], jnp.zeros((spare, width), f32)], axis=0
+            )
+
+        square = jnp.concatenate([first_ref[...], jnp.zeros((taps, LANES - hidden), f32)], axis=1)
+        square = jnp.concatenate([square, jnp.zeros((LANES - taps, LANES), f32)], axis=0)
+        first_taps = square.T[:hidden]
         shape = (most, hidden, 3 * tall)
         out_row = lax.broadcasted_iota(jnp.int32, shape, 0)
         column = lax.broadcasted_iota(jnp.int32, shape, 2)
@@ -277,13 +296,9 @@
         for tap in range(9):
             a, e = tap // 3, tap % 3
             chosen = column == out_row + (a + e * tall)
-            spread = jnp.where(chosen, first_ref[:, tap : tap + 1][None], spread)
+            spread = jnp.where(chosen, first_taps[:, tap : tap + 1][None], spread)
         spread = spread.reshape(most * hidden, 3 * tall)
 
-        field = jnp.concatenate(
-            [low_ref[...], own_ref[...], high_ref[...], jnp.zeros((tall - rows - 2 * HALO, width), f32)],
-            axis=0,
-        )
         state_hi, state_lo = halves(jnp.concatenate(shifted(field), axis=0))
         values = product(halves(spread), state_hi, state_lo)
         live = most
@@ -303,7 +318,8 @@
                     keep(layer + 1, r + i, values[hidden * i : hidden * (i + 1)])
         used = step * live
         weights = halves(banded([last_ref[t : t + 1, :] for t in range(taps)], rows))
-        out_ref[...] = own_ref[...] - product(weights, hi_ref[:used, :], lo_ref[:used, :])
+        change = product(weights, hi_ref[:used, :], lo_ref[:used, :])
+        out_ref[...] = own_ref[...] - (turned(cut(change)) if across else change)
 
     return pl.pallas_call(
         kernel,
@@ -320,21 +336,38 @@
     return [(i, i + shift) for i in range(count) if 0 <= i + shift < count]
 
 
-def from_below(field, axis, count):
-    return lax.ppermute(field[-HALO:], axis, line(count, 1))
-
-
-def from_above(field, axis, count):
-    return lax.ppermute(field[:HALO], axis, line(count, -1))
-
-
 def swap(value, agents, k):
     return lax.ppermute(value, "agent", [(i, i ^ k) for i in range(agents)])
 
 
-def by_row(state):
-    own, voxels = state.shape
-    return state.reshape(own, PX, voxels // PX).transpose(1, 0, 2).reshape(PX, own * (voxels // PX))
+def join(model_state, planar_state, sagittal_state, gradient, pieces, planar_image, sagittal_image):
+    count = len(pieces)
+
+    def kernel(*refs):
+        model, plane, side, first, plane_image, side_image = [r[...] for r in refs[:6]]
+        piece_refs, outs = refs[6 : 6 + count], refs[6 + count :]
+        second = piece_refs[0][...]
+        for ref in piece_refs[1:]:
+            second = second + ref[...].astype(f32)
+        guess = model - 0.5 * first
+        model_image = guess - 0.5 * (second + (guess - model))
+        reflect_model = 2.0 * model_image - model
+        reflect_plane = 2.0 * plane_image - plane
+        reflect_side = 2.0 * side_image - side
+        consensus = 0.5 * reflect_model + 0.25 * reflect_plane + 0.25 * reflect_side
+        outs[0][0] = 0.5 * model + 0.5 * (2.0 * consensus - reflect_model)
+        outs[1][0] = 0.5 * plane + 0.5 * (2.0 * consensus - reflect_plane)
+        outs[2][0] = 0.5 * side + 0.5 * (2.0 * consensus - reflect_side)
+
+    values = (model_state, planar_state, sagittal_state, gradient, planar_image, sagittal_image, *pieces)
+    return pl.pallas_call(
+        kernel,
+        out_shape=[jax.ShapeDtypeStruct((1,) + model_state.shape, f32)] * 3,
+        in_specs=[VMEM] * len(values),
+        out_specs=[VMEM] * 3,
+        compiler_params=params(4),
+        name="join",
+    )(*[onchip(v) for v in values])
 
 
 def body(
@@ -380,37 +413,26 @@
     chip = mask_blocks(view_tile, block_mask)
     sent, anchor, matrix = project_first(parts, chip, agent)
 
-    plane, plane_in, side_in, tile_at = lax.optimization_barrier(
-        (by_row(planar_state), planar_in.T, sagittal_in.T, tile_at)
-    )
-    plane_low = from_below(plane, TILE, tiles)
-    plane_high = from_above(plane, TILE, tiles)
-    side_low = from_below(sagittal_state, "agent", agents)
-    side_high = from_above(sagittal_state, "agent", agents)
+    edge = HALO * LANES
+    sent, plane, side, tile_at = lax.optimization_barrier((sent, planar_state, sagittal_state, tile_at))
+    plane_low = lax.ppermute(plane[:, -edge:], TILE, line(tiles, 1))
+    plane_high = lax.ppermute(plane[:, :edge], TILE, line(tiles, -1))
+    side_low = lax.ppermute(side[-HALO:], "agent", line(agents, 1))
+    side_high = lax.ppermute(side[:HALO], "agent", line(agents, -1))
 
     misfit = gathered(sent)
     total, piece, chip = back_project(misfit, matrix, agent, agents, True)
     pieces = [total] + [swap(piece, agents, k) for k in range(1, agents)]
     sent, gradient = project_next(anchor, pieces, chip, agent)
-    guess = model_state - 0.5 * gradient
-
     misfit = gathered(sent)
     pieces = back_project(misfit, matrix, agent, agents, False)
     pieces = [pieces[0]] + [swap(pieces[k], agents, k) for k in range(1, agents)]
-    gradient = sum(piece.astype(f32) for piece in pieces)
-    model_image = guess - 0.5 * (gradient + (guess - model_state))
-
-    planar_image = by_row(denoise(plane_low, plane, plane_high, plane_in, planar_mid, planar_out, tile_at, tiles))
-    sagittal_image = denoise(side_low, sagittal_state, side_high, side_in, sagittal_mid, sagittal_out, agent, agents)
-
-    reflect_model = 2.0 * model_image - model_state
-    reflect_plane = 2.0 * planar_image - planar_state
-    reflect_side = 2.0 * sagittal_image - sagittal_state
-    consensus = 0.5 * reflect_model + 0.25 * reflect_plane + 0.25 * reflect_side
-    model_next = 0.5 * model_state + 0.5 * (2.0 * consensus - reflect_model)
-    planar_next = 0.5 * planar_state + 0.5 * (2.0 * consensus - reflect_plane)
-    sagittal_next = 0.5 * sagittal_state + 0.5 * (2.0 * consensus - reflect_side)
-    return (model_next[None], planar_next[None], sagittal_next[None])
+    kernels = (planar_in, planar_mid, planar_out)
+    planar_image = denoise(plane_low, planar_state, plane_high, *kernels, tile_at, tiles, True)
+    kernels = (sagittal_in, sagittal_mid, sagittal_out)
+    sagittal_image = denoise(side_low, sagittal_state, side_high, *kernels, agent, agents, False)
+    states = (model_state, planar_state, sagittal_state)
+    return join(*states, gradient, pieces, planar_image, sagittal_image)
 
 
 def solution(mesh):

time: 119 us -> 122 us (1.025); the launches traced: 117 us -> 121 us
  blocking collectives: 11.8 us -> 23.6 us
  waiting for transfers between devices: 22.7 us -> 13.8 us
  local copies, waits for them, and re-layouts: 1.66 us -> 6.89 us
  starting transfers between devices: 53.9 us -> 51.6 us
  other arithmetic: 2.15 us -> 0.84 us
    all_to_all x0 -> x1, blocking collectives: none -> 11.7 us  [gathered(): got = lax.all_to_all(sent.reshape(spread, per, own, LANES), PLANE, 0, 0)]
    all_to_all x2 -> x1, waiting for transfers between devices: 14.1 us -> 7.13 us  [gathered(): got = lax.all_to_all(sent.reshape(spread, per, own, LANES), PLANE, 0, 0)]
    unnamed x21 -> x23, local copies, waits for them, and re-layouts: 0.91 us -> 6.15 us
    all_to_all x2 -> x1, starting transfers between devices: 12.7 us -> 7.63 us  [gathered(): got = lax.all_to_all(sent.reshape(spread, per, own, LANES), PLANE, 0, 0)]
    ppermute x4, starting transfers between devices: 11.8 us -> 13.7 us  [the longest x1 5.82 us: body(): plane_high = lax.ppermute(plane[:, :edge], TILE, line(tiles, -1))]
    ppermute x9, waiting for transfers between devices: 7.17 us -> 5.72 us  [swap(): return lax.ppermute(value, 'agent', [(i, i ^ k) for i in range(agents)])]
    broadcast_in_dim x2 -> x0, other arithmetic: 1.3 us -> none  [body(): return (model_next[None], planar_next[None], sagittal_next[None])]
  transfers between devices with their start and end apart: 18 -> 17, of which waited for: 7 -> 4; matrix products, arithmetic and copies ran while one was open for 1% -> 1% of each run, Pallas kernels for 12% -> 12%
where the time goes in v1:
time: 122 us; the launch traced here: 121 us
  starting transfers between devices  51.6 us (42%)
  blocking collectives  23.6 us (19%)
  Pallas kernels  23.5 us (19%)
  waiting for transfers between devices  13.8 us (11%)
  local copies, waits for them, and re-layouts  6.89 us (6%)
    ppermute x9, starting transfers between devices, swap(): return lax.ppermute(value, 'agent', [(i, i ^ k) for i in range(agents)])  14.1 us
    all_to_all x1, blocking collectives, gathered(): misfit = lax.all_to_all(spreaded, PLANE, 0, 0)  11.8 us
    all_to_all x1, blocking collectives, gathered(): got = lax.all_to_all(sent.reshape(spread, per, own, LANES), PLANE, 0, 0)  11.7 us
    ppermute x2, starting transfers between devices, gathered(): other = lax.ppermute(half, 'zh', [(0, 1), (1, 0)])  11.2 us
    all_to_all x1, starting transfers between devices, gathered(): got = lax.all_to_all(sent.reshape(spread, per, own, LANES), PLANE, 0, 0)  7.63 us
    all_to_all x1, waiting for transfers between devices, gathered(): got = lax.all_to_all(sent.reshape(spread, per, own, LANES), PLANE, 0, 0)  7.13 us
    pallas_call x2, Pallas kernels, denoise(): pl.pallas_call(kernel, out_shape=jax.ShapeDtypeStruct((rows, width), f32)...  6.67 us
    pallas_call x2, Pallas kernels, back_project(): pl.pallas_call(kernel, out_shape=outs, in_specs=[SMEM, VMEM, HBM], out_sp...  6.23 us
  transfers between devices with their start and end apart: 17, of which 4 were waited for; matrix products, arithmetic and copies ran while one was open for 1% of the time, Pallas kernels for 12%

profile of v1, /device:TPU:2, one launch (start us, length us, event | category | flops | bytes accessed | tf_op | source)
XLA Modules:
  0.0 121.2 jit_solution(17742152814285598534)
XLA Ops:
  0.6 0.8 bitcast_convert_fusion.refs_0_
  1.4 1.9 %collective-permute-start = (bf16[8,1024]{1,0:T(8,128)(2,1)S(1)}, bf16[8,1024]{1,0:T(8,128)(2,1)S(1)}, u32[]{:S(2)}, u32[]{:S(2)}) collective-permute-start(bf16[8,1024]{1,0:T(8,128)(2,1)S(1)} %bitcast_convert_fusion.refs_0_), channel_id=1, source_target_pairs={{0,1},{1,0},{2,3},{3,2},{4,5},{5,4},{6,7},{7,6},{8,9},{9,8},{10,11... | collective-permute-start | bytes 49160 | tf_op jit(solution)/shard_map/ppermute | solution.py:340
  3.3 3.3 %collective-permute-start.1 = (bf16[8,1024]{1,0:T(8,128)(2,1)S(1)}, bf16[8,1024]{1,0:T(8,128)(2,1)S(1)}, u32[]{:S(2)}, u32[]{:S(2)}) collective-permute-start(bf16[8,1024]{1,0:T(8,128)(2,1)S(1)} %bitcast_convert_fusion.refs_0_), channel_id=1, source_target_pairs={{0,2},{1,3},{2,0},{3,1},{4,6},{5,7},{6,4},{7,5},{8,10},{9,11},{10,... | collective-permute-start | bytes 49160 | tf_op jit(solution)/shard_map/ppermute | solution.py:340
  6.6 0.0 collective-permute-start.2
  6.6 0.7 copy.16.mask_ref
  7.3 3.8 %mask_blocks.1.refs_4_ = bf16[4,768,1024]{2,1,0:T(8,128)(2,1)S(1)} custom-call(s32[4,1,6,8]{3,2,1,0:T(8,128)S(1)} %copy.16.mask_ref, bf16[4,1,768,1024]{3,2,1,0:T(8,128)(2,1)} %view_ref.1), custom_call_target="tpu_custom_call" | custom-call | tf_op jit(solution)/shard_map/mask_blocks/pallas_call | solution.py:67
  11.1 0.0 copy-start
  11.2 2.6 %copy-done = bf16[4,768,1024]{2,1,0:T(8,128)(2,1)} copy-done((bf16[4,768,1024]{2,1,0:T(8,128)(2,1)}, bf16[4,768,1024]{2,1,0:T(8,128)(2,1)S(1)}, u32[]{:S(2)}) %copy-start) | copy-done | bytes 6291480
  13.8 0.0 collective-permute-done.refs_1_
  13.8 0.0 collective-permute-done.1.refs_2_
  13.8 0.0 collective-permute-done.2.refs_3_
  13.8 0.0 copy-start.1
  13.8 2.8 %copy-done.1 = bf16[4,768,1024]{2,1,0:T(8,128)(2,1)S(1)} copy-done((bf16[4,768,1024]{2,1,0:T(8,128)(2,1)S(1)}, bf16[4,768,1024]{2,1,0:T(8,128)(2,1)}, u32[]{:S(2)}) %copy-start.1) | copy-done | bytes 6291480
  16.6 3.4 %project_first.1 = (bf16[96,8,128]{2,1,0:T(8,128)(2,1)}, f32[32,1024]{1,0:T(8,128)S(1)}, bf16[4,768,1024]{2,1,0:T(8,128)(2,1)}) custom-call(s32[1]{0:T(128)} %bitcast.3.me_ref.at_ref, bf16[8,1024]{1,0:T(8,128)(2,1)S(1)} %bitcast_convert_fusion.refs_0_, bf16[8,1024]{1,0:T(8,128)(2,1)S(1)} %collective-permute-done.refs_1_, ...), custom_call_target="tpu_custom_call" | custom-call | tf_op jit(solution)/shard_map/project_first/pallas_call | solution.py:105
  20.0 7.6 %all-to-all-start = ((bf16[32,3,8,128]{3,2,1,0:T(8,128)(2,1)}), bf16[32,3,8,128]{3,2,1,0:T(8,128)(2,1)S(1)}, u32[]{:S(2)}, u32[]{:S(2)}) async-start(bf16[32,3,8,128]{3,2,1,0:T(8,128)(2,1)} %bitcast.5), calls=%async_computation | async-start | bytes 393216 | tf_op jit(solution)/shard_map/all_to_all | solution.py:404
  27.6 7.1 %all-to-all-done = bf16[32,3,8,128]{3,2,1,0:T(8,128)(2,1)S(1)} async-done(((bf16[32,3,8,128]{3,2,1,0:T(8,128)(2,1)}), bf16[32,3,8,128]{3,2,1,0:T(8,128)(2,1)S(1)}, u32[]{:S(2)}, u32[]{:S(2)}) %all-to-all-start) | async-done | bytes 196640 | tf_op jit(solution)/shard_map/all_to_all | solution.py:404
  34.8 6.5 %collective-permute-start.3 = (f32[3,8,128]{2,1,0:T(8,128)S(1)}, f32[3,8,128]{2,1,0:T(8,128)S(1)}, u32[]{:S(2)}, u32[]{:S(2)}) collective-permute-start(f32[3,8,128]{2,1,0:T(8,128)S(1)} %convert_reduce_fusion.1.half_ref), channel_id=1, source_target_pairs={{0,128},{128,0},{1,129},{129,1},{2,130},{130,2},{3,131},{131,3},{4... | collective-permute-start | bytes 36872 | tf_op jit(solution)/shard_map/ppermute | solution.py:406
  41.3 0.7 dynamic-slice_bitcast_fusion
  42.0 0.9 collective-permute-done.3.other_ref
  43.0 11.8 %all_to_all.20 = bf16[32,3,8,128]{3,2,1,0:T(8,128)(2,1)S(1)} all-to-all(bf16[32,3,8,128]{3,2,1,0:T(8,128)(2,1)S(1)} %spread_misfit.2), channel_id=1, replica_groups=mesh['zh'=2,'x'=4,'y'=4,'core'=2,'agent'=4] {'x','y','core'}, dimensions={0} | all-to-all | bytes 393216 | tf_op jit(solution)/shard_map/all_to_all | solution.py:408
  54.8 3.1 %back_project.2 = (f32[32,1024]{1,0:T(8,128)S(1)}, bf16[32,1024]{1,0:T(8,128)(2,1)S(1)}, bf16[4,768,1024]{2,1,0:T(8,128)(2,1)S(1)}) custom-call(s32[1]{0:T(128)} %bitcast.3.me_ref.at_ref, bf16[96,8,128]{2,1,0:T(8,128)(2,1)S(1)} %bitcast.25, bf16[4,768,1024]{2,1,0:T(8,128)(2,1)} %get-tuple-element.22.matrix_ref), custom_call_target="tpu_custom_call" | custom-call | tf_op jit(solution)/shard_map/back_project/pallas_call | solution.py:193
  57.9 0.2 collective-permute-start.4
  58.1 3.8 %collective-permute-start.5 = (bf16[32,1024]{1,0:T(8,128)(2,1)S(1)}, bf16[32,1024]{1,0:T(8,128)(2,1)S(1)}, u32[]{:S(2)}, u32[]{:S(2)}) collective-permute-start(bf16[32,1024]{1,0:T(8,128)(2,1)S(1)} %get-tuple-element.24), channel_id=1, source_target_pairs={{0,2},{1,3},{2,0},{3,1},{4,6},{5,7},{6,4},{7,5},{8,10},{9,11},{10,... | collective-permute-start | bytes 196616 | tf_op jit(solution)/shard_map/ppermute | solution.py:340
  61.9 0.5 collective-permute-start.6
  62.4 0.0 collective-permute-done.4.refs_1_
  62.4 3.6 %collective-permute-done.5.refs_2_ = bf16[32,1024]{1,0:T(8,128)(2,1)S(1)} collective-permute-done((bf16[32,1024]{1,0:T(8,128)(2,1)S(1)}, bf16[32,1024]{1,0:T(8,128)(2,1)S(1)}, u32[]{:S(2)}, u32[]{:S(2)}) %collective-permute-start.5) | collective-permute-done | bytes 65568 | tf_op jit(solution)/shard_map/ppermute | solution.py:340
  66.0 2.1 %collective-permute-done.6.refs_3_ = bf16[32,1024]{1,0:T(8,128)(2,1)S(1)} collective-permute-done((bf16[32,1024]{1,0:T(8,128)(2,1)S(1)}, bf16[32,1024]{1,0:T(8,128)(2,1)S(1)}, u32[]{:S(2)}, u32[]{:S(2)}) %collective-permute-start.6) | collective-permute-done | bytes 65568 | tf_op jit(solution)/shard_map/ppermute | solution.py:340
  68.1 0.0 copy-start.9
  68.1 0.0 copy-start.10
  68.1 0.0 copy-start.6
  68.2 1.9 %project_next.1 = (bf16[96,8,128]{2,1,0:T(8,128)(2,1)S(1)}, f32[8,1024]{1,0:T(8,128)S(1)}) custom-call(s32[1]{0:T(128)} %bitcast.3.me_ref.at_ref, f32[32,1024]{1,0:T(8,128)S(1)} %get-tuple-element.19.anchor_ref, f32[32,1024]{1,0:T(8,128)S(1)} %get-tuple-element.23.refs_0_, bf16[32,1024]{1,0:T(8,128)(2,1)S(1)} %collective-permute-done.4.refs_1_, ...), custom_call_target="tpu_custom_call" | custom-call | tf_op jit(solution)/shard_map/project_next/pallas_call | solution.py:136
  70.1 11.7 %all_to_all.21 = bf16[32,3,8,128]{3,2,1,0:T(8,128)(2,1)S(1)} all-to-all(bf16[32,3,8,128]{3,2,1,0:T(8,128)(2,1)S(1)} %bitcast.32), channel_id=1, replica_groups=mesh['zh'=2,'x'=4,'y'=4,'core'=2,'agent'=4] {'x','y','core'}, dimensions={0} | all-to-all | bytes 393216 | tf_op jit(solution)/shard_map/all_to_all | solution.py:404
  81.9 4.7 %collective-permute-start.11 = (f32[3,8,128]{2,1,0:T(8,128)S(1)}, f32[3,8,128]{2,1,0:T(8,128)S(1)}, u32[]{:S(2)}, u32[]{:S(2)}) collective-permute-start(f32[3,8,128]{2,1,0:T(8,128)S(1)} %convert_reduce_fusion.half_ref), channel_id=1, source_target_pairs={{0,128},{128,0},{1,129},{129,1},{2,130},{130,2},{3,131},{131,3},{4... | collective-permute-start | bytes 36872 | tf_op jit(solution)/shard_map/ppermute | solution.py:406
  86.6 0.0 copy-done.2
  86.6 1.3 %collective-permute-start.10 = (f32[5,1024]{1,0:T(8,128)S(1)}, f32[5,1024]{1,0:T(8,128)S(1)}, u32[]{:S(2)}, u32[]{:S(2)}) collective-permute-start(f32[5,1024]{1,0:T(8,128)S(1)} %get-tuple-element.35), channel_id=1, source_target_pairs={{1,0},{2,1},{3,2},{5,4},{6,5},{7,6},{9,8},{10,9},{11,10},{13,12},{... | collective-permute-start | bytes 61448 | tf_op jit(solution)/shard_map/ppermute | solution.py:421
  87.9 4.5 %collective-permute-start.9 = (f32[5,1024]{1,0:T(8,128)S(1)}, f32[5,1024]{1,0:T(8,128)S(1)}, u32[]{:S(2)}, u32[]{:S(2)}) collective-permute-start(f32[5,1024]{1,0:T(8,128)S(1)} %get-tuple-element.36), channel_id=1, source_target_pairs={{0,1},{1,2},{2,3},{4,5},{5,6},{6,7},{8,9},{9,10},{10,11},{12,13},{... | collective-permute-start | bytes 61448 | tf_op jit(solution)/shard_map/ppermute | solution.py:420
  92.4 0.0 collective-permute-done.11.other_ref
  92.4 0.7 spread_misfit.3
  93.1 5.0 %all-to-all-start.3 = ((bf16[32,3,8,128]{3,2,1,0:T(8,128)(2,1)}), bf16[32,3,8,128]{3,2,1,0:T(8,128)(2,1)S(1)}, u32[]{:S(2)}, u32[]{:S(2)}) async-start(bf16[32,3,8,128]{3,2,1,0:T(8,128)(2,1)} %spread_misfit.3), calls=%async_computation.3 | async-start | bytes 393216 | tf_op jit(solution)/shard_map/all_to_all | solution.py:408
  98.2 0.0 copy-done.3
  98.2 2.0 %collective-permute-start.7 = (f32[8,640]{1,0:T(8,128)S(1)}, f32[8,640]{1,0:T(8,128)S(1)}, u32[]{:S(2)}, u32[]{:S(2)}) collective-permute-start(f32[8,640]{1,0:T(8,128)S(1)} %get-tuple-element.38), channel_id=1, source_target_pairs={{0,4},{4,8},{8,12},{12,16},{16,20},{20,24},{24,28},{28,32},{32,36}... | collective-permute-start | bytes 61448 | tf_op jit(solution)/shard_map/ppermute | solution.py:418
  100.2 5.8 %collective-permute-start.8 = (f32[8,640]{1,0:T(8,128)S(1)}, f32[8,640]{1,0:T(8,128)S(1)}, u32[]{:S(2)}, u32[]{:S(2)}) collective-permute-start(f32[8,640]{1,0:T(8,128)S(1)} %get-tuple-element.37), channel_id=1, source_target_pairs={{4,0},{8,4},{12,8},{16,12},{20,16},{24,20},{28,24},{32,28},{36,32}... | collective-permute-start | bytes 61448 | tf_op jit(solution)/shard_map/ppermute | solution.py:419
  106.1 0.0 all-to-all-done.3
  106.1 3.1 %back_project.3 = (f32[8,1024]{1,0:T(8,128)S(1)}, bf16[8,1024]{1,0:T(8,128)(2,1)S(1)}, bf16[8,1024]{1,0:T(8,128)(2,1)S(1)}, bf16[8,1024]{1,0:T(8,128)(2,1)S(1)}) custom-call(s32[1]{0:T(128)} %bitcast.3.me_ref.at_ref, bf16[96,8,128]{2,1,0:T(8,128)(2,1)S(1)} %bitcast.24, bf16[4,768,1024]{2,1,0:T(8,128)(2,1)} %get-tuple-element.22.matrix_ref), custom_call_target="tpu_custom_call" | custom-call | tf_op jit(solution)/shard_map/back_project/pallas_call | solution.py:193
  109.2 1.3 %collective-permute-start.12 = (bf16[8,1024]{1,0:T(8,128)(2,1)S(1)}, bf16[8,1024]{1,0:T(8,128)(2,1)S(1)}, u32[]{:S(2)}, u32[]{:S(2)}) collective-permute-start(bf16[8,1024]{1,0:T(8,128)(2,1)S(1)} %get-tuple-element.32), channel_id=1, source_target_pairs={{0,1},{1,0},{2,3},{3,2},{4,5},{5,4},{6,7},{7,6},{8,9},{9,8},{10,11... | collective-permute-start | bytes 49160 | tf_op jit(solution)/shard_map/ppermute | solution.py:340
  110.5 0.0 collective-permute-done.10.high_ref
  110.5 0.5 collective-permute-start.13
  111.0 0.0 collective-permute-done.9.low_ref
  111.0 2.7 %collective-permute-start.14 = (bf16[8,1024]{1,0:T(8,128)(2,1)S(1)}, bf16[8,1024]{1,0:T(8,128)(2,1)S(1)}, u32[]{:S(2)}, u32[]{:S(2)}) collective-permute-start(bf16[8,1024]{1,0:T(8,128)(2,1)S(1)} %get-tuple-element.34), channel_id=1, source_target_pairs={{0,3},{1,2},{2,1},{3,0},{4,7},{5,6},{6,5},{7,4},{8,11},{9,10},{10,... | collective-permute-start | bytes 49160 | tf_op jit(solution)/shard_map/ppermute | solution.py:340
  113.7 0.0 copy-done.4
  113.7 0.0 copy-done.7
  113.7 0.0 copy-done.8
  113.7 3.3 %denoise.3.refs_5_ = f32[8,1024]{1,0:T(8,128)S(1)} custom-call(s32[1]{0:T(128)} %bitcast.3.me_ref.at_ref, f32[5,1024]{1,0:T(8,128)S(1)} %collective-permute-done.9.low_ref, f32[8,1024]{1,0:T(8,128)S(1)} %bitcast.27, f32[5,1024]{1,0:T(8,128)S(1)} %collective-permute-done.10.high_ref, f32[9,16]{1,0:T(8,128)S(1)} %copy-done.7, f32[3,9,16,16]{3,2,1,0:T(8,128)S(1)} %copy-done.4, ...), custom_call_target="tpu_custom_call" | custom-call | tf_op jit(solution)/shard_map/denoise/pallas_call | solution.py:324
  117.0 0.0 collective-permute-done.7.low_ref
  117.0 0.0 collective-permute-done.8.high_ref
  117.0 0.0 copy-done.5
  117.1 0.0 copy-done.9
  117.1 0.0 copy-done.10
  117.1 3.4 %denoise.2.refs_4_ = f32[8,1024]{1,0:T(8,128)S(1)} custom-call(s32[1]{0:T(128)} %bitcast.4.at_ref, f32[8,640]{1,0:T(8,128)S(1)} %collective-permute-done.7.low_ref, f32[8,1024]{1,0:T(8,128)S(1)} %bitcast.30, f32[8,640]{1,0:T(8,128)S(1)} %collective-permute-done.8.high_ref, f32[9,16]{1,0:T(8,128)S(1)} %copy-done.9, f32[3,9,16,16]{3,2,1,0:T(8,128)S(1)} %copy-done.5, ...), custom_call_target="tpu_custom_call" | custom-call | tf_op jit(solution)/shard_map/denoise/pallas_call | solution.py:324
  120.4 0.0 collective-permute-done.12.refs_7_
  120.5 0.0 collective-permute-done.13.refs_8_
  120.5 0.0 collective-permute-done.14.refs_9_
  120.5 0.0 copy-done.6
  120.5 0.7 join.1
  (11 shorter events, 0.1 us)
Async XLA Ops:
  1.4 12.4 %collective-permute-start = (bf16[8,1024]{1,0:T(8,128)(2,1)S(1)}, bf16[8,1024]{1,0:T(8,128)(2,1)S(1)}, u32[]{:S(2)}, u32[]{:S(2)}) collective-permute-start(bf16[8,1024]{1,0:T(8,128)(2,1)S(1)} %bitcast_convert_fusion.refs_0_), channel_id=1, source_target_pairs={{0,1},{1,0},{2,3},{3,2},{4,5},{5,4},{6,7},{7,6},{8,9},{9,8},{10,11... | collective-permute-start | bytes 49160 | tf_op jit(solution)/shard_map/ppermute | solution.py:340
  3.3 10.5 %collective-permute-start.1 = (bf16[8,1024]{1,0:T(8,128)(2,1)S(1)}, bf16[8,1024]{1,0:T(8,128)(2,1)S(1)}, u32[]{:S(2)}, u32[]{:S(2)}) collective-permute-start(bf16[8,1024]{1,0:T(8,128)(2,1)S(1)} %bitcast_convert_fusion.refs_0_), channel_id=1, source_target_pairs={{0,2},{1,3},{2,0},{3,1},{4,6},{5,7},{6,4},{7,5},{8,10},{9,11},{10,... | collective-permute-start | bytes 49160 | tf_op jit(solution)/shard_map/ppermute | solution.py:340
  6.6 7.2 %collective-permute-start.2 = (bf16[8,1024]{1,0:T(8,128)(2,1)S(1)}, bf16[8,1024]{1,0:T(8,128)(2,1)S(1)}, u32[]{:S(2)}, u32[]{:S(2)}) collective-permute-start(bf16[8,1024]{1,0:T(8,128)(2,1)S(1)} %bitcast_convert_fusion.refs_0_), channel_id=1, source_target_pairs={{0,3},{1,2},{2,1},{3,0},{4,7},{5,6},{6,5},{7,4},{8,11},{9,10},{10,... | collective-permute-start | bytes 49160 | tf_op jit(solution)/shard_map/ppermute | solution.py:340
  11.1 2.6 %copy-start = (bf16[4,768,1024]{2,1,0:T(8,128)(2,1)}, bf16[4,768,1024]{2,1,0:T(8,128)(2,1)S(1)}, u32[]{:S(2)}) copy-start(bf16[4,768,1024]{2,1,0:T(8,128)(2,1)S(1)} %mask_blocks.1.refs_4_) | copy-start | bytes 18874372
  13.8 2.8 %copy-start.1 = (bf16[4,768,1024]{2,1,0:T(8,128)(2,1)S(1)}, bf16[4,768,1024]{2,1,0:T(8,128)(2,1)}, u32[]{:S(2)}) copy-start(bf16[4,768,1024]{2,1,0:T(8,128)(2,1)} %copy-done) | copy-start | bytes 18874372
  20.0 14.8 %all-to-all-start = ((bf16[32,3,8,128]{3,2,1,0:T(8,128)(2,1)}), bf16[32,3,8,128]{3,2,1,0:T(8,128)(2,1)S(1)}, u32[]{:S(2)}, u32[]{:S(2)}) async-start(bf16[32,3,8,128]{3,2,1,0:T(8,128)(2,1)} %bitcast.5), calls=%async_computation | async-start | bytes 393216 | tf_op jit(solution)/shard_map/all_to_all | solution.py:404
  34.8 8.1 %collective-permute-start.3 = (f32[3,8,128]{2,1,0:T(8,128)S(1)}, f32[3,8,128]{2,1,0:T(8,128)S(1)}, u32[]{:S(2)}, u32[]{:S(2)}) collective-permute-start(f32[3,8,128]{2,1,0:T(8,128)S(1)} %convert_reduce_fusion.1.half_ref), channel_id=1, source_target_pairs={{0,128},{128,0},{1,129},{129,1},{2,130},{130,2},{3,131},{131,3},{4... | collective-permute-start | bytes 36872 | tf_op jit(solution)/shard_map/ppermute | solution.py:406
  54.8 31.8 %copy-start.2 = (f32[1,8,1024]{2,1,0:T(8,128)S(1)}, f32[1,8,1024]{2,1,0:T(8,128)}, u32[]{:S(2)}) copy-start(f32[1,8,1024]{2,1,0:T(8,128)} %param.19) | copy-start | bytes 98308
  54.8 43.4 %copy-start.3 = (f32[1,8,1024]{2,1,0:T(8,128)S(1)}, f32[1,8,1024]{2,1,0:T(8,128)}, u32[]{:S(2)}) copy-start(f32[1,8,1024]{2,1,0:T(8,128)} %param.18) | copy-start | bytes 98308
  57.9 4.5 %collective-permute-start.4 = (bf16[32,1024]{1,0:T(8,128)(2,1)S(1)}, bf16[32,1024]{1,0:T(8,128)(2,1)S(1)}, u32[]{:S(2)}, u32[]{:S(2)}) collective-permute-start(bf16[32,1024]{1,0:T(8,128)(2,1)S(1)} %get-tuple-element.24), channel_id=1, source_target_pairs={{0,1},{1,0},{2,3},{3,2},{4,5},{5,4},{6,7},{7,6},{8,9},{9,8},{10,11... | collective-permute-start | bytes 196616 | tf_op jit(solution)/shard_map/ppermute | solution.py:340
  58.1 7.8 %collective-permute-start.5 = (bf16[32,1024]{1,0:T(8,128)(2,1)S(1)}, bf16[32,1024]{1,0:T(8,128)(2,1)S(1)}, u32[]{:S(2)}, u32[]{:S(2)}) collective-permute-start(bf16[32,1024]{1,0:T(8,128)(2,1)S(1)} %get-tuple-element.24), channel_id=1, source_target_pairs={{0,2},{1,3},{2,0},{3,1},{4,6},{5,7},{6,4},{7,5},{8,10},{9,11},{10,... | collective-permute-start | bytes 196616 | tf_op jit(solution)/shard_map/ppermute | solution.py:340
  61.9 6.2 %collective-permute-start.6 = (bf16[32,1024]{1,0:T(8,128)(2,1)S(1)}, bf16[32,1024]{1,0:T(8,128)(2,1)S(1)}, u32[]{:S(2)}, u32[]{:S(2)}) collective-permute-start(bf16[32,1024]{1,0:T(8,128)(2,1)S(1)} %get-tuple-element.24), channel_id=1, source_target_pairs={{0,3},{1,2},{2,1},{3,0},{4,7},{5,6},{6,5},{7,4},{8,11},{9,10},{10,... | collective-permute-start | bytes 196616 | tf_op jit(solution)/shard_map/ppermute | solution.py:340
  68.1 45.6 %copy-start.4 = (f32[3,9,16,16]{3,2,1,0:T(8,128)S(1)}, f32[3,9,16,16]{3,2,1,0:T(8,128)}, u32[]{:S(2)}) copy-start(f32[3,9,16,16]{3,2,1,0:T(8,128)} %mid_ref.3) | copy-start | bytes 82948
  68.1 45.6 %copy-start.7 = (f32[9,16]{1,0:T(8,128)S(1)}, f32[9,16]{1,0:T(8,128)}, u32[]{:S(2)}) copy-start(f32[9,16]{1,0:T(8,128)} %first_ref.3) | copy-start | bytes 1732
  68.1 45.6 %copy-start.8 = (f32[9,16]{1,0:T(8,128)S(1)}, f32[9,16]{1,0:T(8,128)}, u32[]{:S(2)}) copy-start(f32[9,16]{1,0:T(8,128)} %last_ref.3) | copy-start | bytes 1732
  68.1 48.9 %copy-start.5 = (f32[3,9,16,16]{3,2,1,0:T(8,128)S(1)}, f32[3,9,16,16]{3,2,1,0:T(8,128)}, u32[]{:S(2)}) copy-start(f32[3,9,16,16]{3,2,1,0:T(8,128)} %mid_ref.2) | copy-start | bytes 82948
  68.1 48.9 %copy-start.9 = (f32[9,16]{1,0:T(8,128)S(1)}, f32[9,16]{1,0:T(8,128)}, u32[]{:S(2)}) copy-start(f32[9,16]{1,0:T(8,128)} %first_ref.2) | copy-start | bytes 1732
  68.1 48.9 %copy-start.10 = (f32[9,16]{1,0:T(8,128)S(1)}, f32[9,16]{1,0:T(8,128)}, u32[]{:S(2)}) copy-start(f32[9,16]{1,0:T(8,128)} %last_ref.2) | copy-start | bytes 1732
  68.1 52.3 %copy-start.6 = (f32[1,8,1024]{2,1,0:T(8,128)S(1)}, f32[1,8,1024]{2,1,0:T(8,128)}, u32[]{:S(2)}) copy-start(f32[1,8,1024]{2,1,0:T(8,128)} %param.17) | copy-start | bytes 98308
  81.9 10.6 %collective-permute-start.11 = (f32[3,8,128]{2,1,0:T(8,128)S(1)}, f32[3,8,128]{2,1,0:T(8,128)S(1)}, u32[]{:S(2)}, u32[]{:S(2)}) collective-permute-start(f32[3,8,128]{2,1,0:T(8,128)S(1)} %convert_reduce_fusion.half_ref), channel_id=1, source_target_pairs={{0,128},{128,0},{1,129},{129,1},{2,130},{130,2},{3,131},{131,3},{4... | collective-permute-start | bytes 36872 | tf_op jit(solution)/shard_map/ppermute | solution.py:406
  86.6 23.9 %collective-permute-start.10 = (f32[5,1024]{1,0:T(8,128)S(1)}, f32[5,1024]{1,0:T(8,128)S(1)}, u32[]{:S(2)}, u32[]{:S(2)}) collective-permute-start(f32[5,1024]{1,0:T(8,128)S(1)} %get-tuple-element.35), channel_id=1, source_target_pairs={{1,0},{2,1},{3,2},{5,4},{6,5},{7,6},{9,8},{10,9},{11,10},{13,12},{... | collective-permute-start | bytes 61448 | tf_op jit(solution)/shard_map/ppermute | solution.py:421
  87.9 23.2 %collective-permute-start.9 = (f32[5,1024]{1,0:T(8,128)S(1)}, f32[5,1024]{1,0:T(8,128)S(1)}, u32[]{:S(2)}, u32[]{:S(2)}) collective-permute-start(f32[5,1024]{1,0:T(8,128)S(1)} %get-tuple-element.36), channel_id=1, source_target_pairs={{0,1},{1,2},{2,3},{4,5},{5,6},{6,7},{8,9},{9,10},{10,11},{12,13},{... | collective-permute-start | bytes 61448 | tf_op jit(solution)/shard_map/ppermute | solution.py:420
  93.1 12.9 %all-to-all-start.3 = ((bf16[32,3,8,128]{3,2,1,0:T(8,128)(2,1)}), bf16[32,3,8,128]{3,2,1,0:T(8,128)(2,1)S(1)}, u32[]{:S(2)}, u32[]{:S(2)}) async-start(bf16[32,3,8,128]{3,2,1,0:T(8,128)(2,1)} %spread_misfit.3), calls=%async_computation.3 | async-start | bytes 393216 | tf_op jit(solution)/shard_map/all_to_all | solution.py:408
  98.2 18.8 %collective-permute-start.7 = (f32[8,640]{1,0:T(8,128)S(1)}, f32[8,640]{1,0:T(8,128)S(1)}, u32[]{:S(2)}, u32[]{:S(2)}) collective-permute-start(f32[8,640]{1,0:T(8,128)S(1)} %get-tuple-element.38), channel_id=1, source_target_pairs={{0,4},{4,8},{8,12},{12,16},{16,20},{20,24},{24,28},{28,32},{32,36}... | collective-permute-start | bytes 61448 | tf_op jit(solution)/shard_map/ppermute | solution.py:418
  100.2 16.8 %collective-permute-start.8 = (f32[8,640]{1,0:T(8,128)S(1)}, f32[8,640]{1,0:T(8,128)S(1)}, u32[]{:S(2)}, u32[]{:S(2)}) collective-permute-start(f32[8,640]{1,0:T(8,128)S(1)} %get-tuple-element.37), channel_id=1, source_target_pairs={{4,0},{8,4},{12,8},{16,12},{20,16},{24,20},{28,24},{32,28},{36,32}... | collective-permute-start | bytes 61448 | tf_op jit(solution)/shard_map/ppermute | solution.py:419
  109.2 11.2 %collective-permute-start.12 = (bf16[8,1024]{1,0:T(8,128)(2,1)S(1)}, bf16[8,1024]{1,0:T(8,128)(2,1)S(1)}, u32[]{:S(2)}, u32[]{:S(2)}) collective-permute-start(bf16[8,1024]{1,0:T(8,128)(2,1)S(1)} %get-tuple-element.32), channel_id=1, source_target_pairs={{0,1},{1,0},{2,3},{3,2},{4,5},{5,4},{6,7},{7,6},{8,9},{9,8},{10,11... | collective-permute-start | bytes 49160 | tf_op jit(solution)/shard_map/ppermute | solution.py:340
  110.5 10.0 %collective-permute-start.13 = (bf16[8,1024]{1,0:T(8,128)(2,1)S(1)}, bf16[8,1024]{1,0:T(8,128)(2,1)S(1)}, u32[]{:S(2)}, u32[]{:S(2)}) collective-permute-start(bf16[8,1024]{1,0:T(8,128)(2,1)S(1)} %get-tuple-element.33), channel_id=1, source_target_pairs={{0,2},{1,3},{2,0},{3,1},{4,6},{5,7},{6,4},{7,5},{8,10},{9,11},{10,... | collective-permute-start | bytes 49160 | tf_op jit(solution)/shard_map/ppermute | solution.py:340
  111.0 9.4 %collective-permute-start.14 = (bf16[8,1024]{1,0:T(8,128)(2,1)S(1)}, bf16[8,1024]{1,0:T(8,128)(2,1)S(1)}, u32[]{:S(2)}, u32[]{:S(2)}) collective-permute-start(bf16[8,1024]{1,0:T(8,128)(2,1)S(1)} %get-tuple-element.34), channel_id=1, source_target_pairs={{0,3},{1,2},{2,1},{3,0},{4,7},{5,6},{6,5},{7,4},{8,11},{9,10},{10,... | collective-permute-start | bytes 49160 | tf_op jit(solution)/shard_map/ppermute | solution.py:340

commit v2 on v1

--- a/solution.py
+++ b/solution.py
@@ -10,6 +10,7 @@
 HALO = 5
 LANES = 128
 SPLIT = 2
+KEPT = 3
 PLANE = ("x", "y", "core")
 TILE = ("zh",) + PLANE
 
@@ -31,18 +32,11 @@
 
 
 def fetch(source, target, sems):
-    views, bins, _ = target.shape
-    rows = bins // SPLIT
     copies = []
-    for v in range(views):
-        for h in range(SPLIT):
-            copy = pltpu.make_async_copy(
-                source.at[v, pl.ds(h * rows, rows)],
-                target.at[v, pl.ds(h * rows, rows)],
-                sems.at[v * SPLIT + h],
-            )
-            copy.start()
-            copies.append((v, h * rows, copy))
+    for i in range(target.shape[0]):
+        copy = pltpu.make_async_copy(source.at[i], target.at[i], sems.at[i])
+        copy.start()
+        copies.append(copy)
     return copies
 
 
@@ -53,116 +47,130 @@
 def mask_blocks(view_tile, mask):
     views, _, bins, voxels = view_tile.shape
     rows = bins // SPLIT
-
-    def kernel(mask_ref, view_ref, chip_ref, sems):
-        for v, first, copy in fetch(view_ref.at[:, 0], chip_ref, sems):
-            copy.wait()
-            for j in range(first, first + rows, LANES):
+    pieces = views * SPLIT
+
+    def kernel(mask_ref, view_ref, kept_ref, rest_ref, sems):
+        places = [kept_ref.at[i] for i in range(KEPT)] + [rest_ref.at[i] for i in range(pieces - KEPT)]
+        copies = []
+        for i, place in enumerate(places):
+            source = view_ref.at[i // SPLIT, 0, pl.ds(i % SPLIT * rows, rows)]
+            copies.append(pltpu.make_async_copy(source, place, sems.at[i]))
+            copies[-1].start()
+        for i, place in enumerate(places):
+            copies[i].wait()
+            for j in range(rows // LANES):
                 for k in range(voxels // LANES):
-                    keep = jnp.full((16, LANES), mask_ref[v, 0, j // LANES, k].astype(f32)).astype(bf16)
-                    at = (v, slice(j, j + LANES), slice(k * LANES, (k + 1) * LANES))
-                    block = chip_ref[at].reshape(8, 16, LANES) * keep[None]
-                    chip_ref[at] = block.reshape(LANES, LANES)
-
-    return pl.pallas_call(
-        kernel,
-        out_shape=pltpu.VMEM((views, bins, voxels), bf16),
+                    empty = mask_ref[i // SPLIT, i % SPLIT * (rows // LANES) + j, 0, k] == 0
+                    at = (slice(j * LANES, (j + 1) * LANES), slice(k * LANES, (k + 1) * LANES))
+
+                    @pl.when(empty)
+                    def _(place=place, at=at):
+                        place[at] = jnp.zeros((LANES, LANES), bf16)
+
+    return pl.pallas_call(
+        kernel,
+        out_shape=[pltpu.VMEM((n, rows, voxels), bf16) for n in (KEPT, pieces - KEPT)],
         in_specs=[SMEM, HBM],
-        out_specs=VMEM,
-        scratch_shapes=[pltpu.SemaphoreType.DMA((views * SPLIT,))],
+        out_specs=[VMEM, VMEM],
+        scratch_shapes=[pltpu.SemaphoreType.DMA((pieces,))],
         compiler_params=params(16),
         name="mask_blocks",
-    )(mask, offchip(view_tile))
-
-
-def project_tiles(low, matrix_ref, out_ref):
-    views, bins, _ = matrix_ref.shape
-    groups, blocks = low.shape[0] // 8, bins // LANES
-    for v in range(views):
+    )(offchip(mask), offchip(view_tile))
+
+
+def piece_list(*refs):
+    return [(ref, i) for ref in refs for i in range(ref.shape[0])]
+
+
+def project_tiles(low, pieces, out_ref):
+    groups = low.shape[0] // 8
+    for n, (ref, i) in enumerate(pieces):
         result = lax.dot_general(
-            low, matrix_ref[v], (((1,), (1,)), ((), ())), preferred_element_type=f32
+            low, ref[i], (((1,), (1,)), ((), ())), preferred_element_type=f32
         ).astype(bf16)
+        blocks = ref.shape[1] // LANES
         for g in range(groups):
             for j in range(blocks):
-                out_ref[(v * groups + g) * blocks + j] = result[8 * g : 8 * g + 8, j * LANES : (j + 1) * LANES]
-
-
-def project_first(parts, matrix, me):
+                at = (n // SPLIT * groups + g) * (SPLIT * blocks) + n % SPLIT * blocks + j
+                out_ref[at] = result[8 * g : 8 * g + 8, j * LANES : (j + 1) * LANES]
+
+
+def project_first(parts, kept, rest, me):
     own, voxels = parts[0].shape
     groups = len(parts)
-    views, bins, _ = matrix.shape
+    tiles = (kept.shape[0] + rest.shape[0]) * groups * kept.shape[1] // LANES
 
     def kernel(me_ref, *refs):
-        part_refs, (matrix_ref, out_ref, anchor_ref, main_ref, sems) = refs[:groups], refs[groups:]
-        copies = fetch(matrix_ref, main_ref, sems)
+        part_refs, (kept_ref, rest_ref, out_ref, anchor_ref, main_ref, sems) = refs[:groups], refs[groups:]
+        copies = fetch(rest_ref, main_ref, sems)
         for k in range(groups):
             first = pl.multiple_of(jnp.bitwise_xor(me_ref[0], k) * own, own)
-            anchor_ref[pl.ds(first, own), :] = part_refs[k][...].astype(f32)
-        project_tiles(anchor_ref[...].astype(bf16), matrix_ref, out_ref)
-        for *_, copy in copies:
+            anchor_ref[pl.ds(first, own), :] = part_refs[k][...]
+        project_tiles(anchor_ref[...].astype(bf16), piece_list(kept_ref, rest_ref), out_ref)
+        for copy in copies:
             copy.wait()
 
     return pl.pallas_call(
         kernel,
         out_shape=[
-            jax.ShapeDtypeStruct((views * groups * bins // LANES, own, LANES), bf16),
+            jax.ShapeDtypeStruct((tiles, own, LANES), bf16),
             jax.ShapeDtypeStruct((groups * own, voxels), f32),
-            pltpu.HBM(matrix.shape, bf16),
+            pltpu.HBM(rest.shape, bf16),
         ],
-        in_specs=[SMEM] + [VMEM] * (groups + 1),
+        in_specs=[SMEM] + [VMEM] * (groups + 2),
         out_specs=[VMEM, VMEM, HBM],
-        scratch_shapes=[pltpu.SemaphoreType.DMA((views * SPLIT,))],
+        scratch_shapes=[pltpu.SemaphoreType.DMA((rest.shape[0],))],
         compiler_params=params(16),
         name="project_first",
-    )(me, *[onchip(p) for p in parts], onchip(matrix))
-
-
-def project_next(anchor, pieces, matrix, me):
+    )(me, *[onchip(p) for p in parts], onchip(kept), onchip(rest))
+
+
+def project_next(anchor, pieces, kept, rest, me):
     slices, voxels = anchor.shape
-    views, bins, _ = matrix.shape
     own = 8
     count = len(pieces)
+    tiles = (kept.shape[0] + rest.shape[0]) * (slices // own) * kept.shape[1] // LANES
 
     def kernel(me_ref, anchor_ref, *refs):
-        piece_refs, (matrix_ref, out_ref, own_ref, gradient_ref) = refs[:count], refs[count:]
+        piece_refs, (kept_ref, rest_ref, out_ref, own_ref, gradient_ref) = refs[:count], refs[count:]
         gradient = piece_refs[0][...]
         for ref in piece_refs[1:]:
             gradient = gradient + ref[...].astype(f32)
         gradient_ref[...] = gradient
         low = (anchor_ref[...] - 0.5 * gradient).astype(bf16)
         own_ref[...] = gradient_ref[pl.ds(pl.multiple_of(me_ref[0] * own, own), own), :]
-        project_tiles(low, matrix_ref, out_ref)
+        project_tiles(low, piece_list(kept_ref, rest_ref), out_ref)
 
     return pl.pallas_call(
         kernel,
         out_shape=[
-            jax.ShapeDtypeStruct((views * slices // own * bins // LANES, own, LANES), bf16),
+            jax.ShapeDtypeStruct((tiles, own, LANES), bf16),
             jax.ShapeDtypeStruct((own, voxels), f32),
         ],
-        in_specs=[SMEM] + [VMEM] * (count + 2),
+        in_specs=[SMEM] + [VMEM] * (count + 3),
         out_specs=[VMEM, VMEM],
         scratch_shapes=[pltpu.VMEM((slices, voxels), f32)],
         compiler_params=params(16),
         name="project_next",
-    )(me, onchip(anchor), *[onchip(p) for p in pieces], onchip(matrix))
-
-
-def back_project(misfit, matrix, me, groups, whole):
-    views, bins, voxels = matrix.shape
+    )(me, onchip(anchor), *[onchip(p) for p in pieces], onchip(kept), onchip(rest))
+
+
+def back_project(misfit, kept, main, me, groups, whole):
+    rows, voxels = kept.shape[1:]
     own = misfit.shape[1]
-    blocks = bins // LANES
-    rows = bins // SPLIT
-
-    def kernel(me_ref, misfit_ref, matrix_ref, *refs):
-        *outs, chip_ref, sems = refs if whole else refs[:-3] + refs[-2:]
+    blocks = rows // LANES
+
+    def kernel(me_ref, misfit_ref, kept_ref, main_ref, *refs):
+        *outs, rest_ref, sems = refs if whole else refs[:-3] + refs[-2:]
+        copies = [None] * KEPT + fetch(main_ref, rest_ref, sems)
         total = None
-        for v, first, copy in fetch(matrix_ref, chip_ref, sems):
+        for n, (ref, i) in enumerate(piece_list(kept_ref, rest_ref)):
             left = jnp.concatenate(
                 [
                     jnp.concatenate(
                         [
-                            misfit_ref[(v * groups + g) * blocks + j].astype(f32)
-                            for j in range(first // LANES, (first + rows) // LANES)
+                            misfit_ref[(n // SPLIT * groups + g) * (SPLIT * blocks) + n % SPLIT * blocks + j].astype(f32)
+                            for j in range(blocks)
                         ],
                         axis=1,
                     )
@@ -170,8 +178,9 @@
                 ],
                 axis=0,
             ).astype(bf16)
-            copy.wait()
-            part = jnp.dot(left, chip_ref[v, first : first + rows, :], preferred_element_type=f32)
+            if copies[n] is not None:
+                copies[n].wait()
+            part = jnp.dot(left, ref[i], preferred_element_type=f32)
             total = part if total is None else total + part
         if whole:
             outs[0][...] = total
@@ -185,20 +194,20 @@
 
     if whole:
         outs = [jax.ShapeDtypeStruct((groups * own, voxels), t) for t in (f32, bf16)]
-        outs.append(pltpu.VMEM(matrix.shape, bf16))
+        outs.append(pltpu.VMEM(main.shape, bf16))
         scratch = []
     else:
         outs = [jax.ShapeDtypeStruct((own, voxels), f32 if k == 0 else bf16) for k in range(groups)]
-        scratch = [pltpu.VMEM((groups * own, voxels), f32), pltpu.VMEM(matrix.shape, bf16)]
+        scratch = [pltpu.VMEM((groups * own, voxels), f32), pltpu.VMEM(main.shape, bf16)]
     return pl.pallas_call(
         kernel,
         out_shape=outs,
-        in_specs=[SMEM, VMEM, HBM],
+        in_specs=[SMEM, VMEM, VMEM, HBM],
         out_specs=[VMEM] * len(outs),
-        scratch_shapes=scratch + [pltpu.SemaphoreType.DMA((views * SPLIT,))],
+        scratch_shapes=scratch + [pltpu.SemaphoreType.DMA((main.shape[0],))],
         compiler_params=params(16),
         name="back_project",
-    )(me, onchip(misfit), offchip(matrix))
+    )(me, onchip(misfit), onchip(kept), offchip(main))
 
 
 def spread_misfit(half, other, sino, weight, copies):
@@ -336,8 +345,8 @@
     return [(i, i + shift) for i in range(count) if 0 <= i + shift < count]
 
 
-def swap(value, agents, k):
-    return lax.ppermute(value, "agent", [(i, i ^ k) for i in range(agents)])
+def swap(value, count, k, axis="agent"):
+    return lax.ppermute(value, axis, [(i, i ^ k) for i in range(count)])
 
 
 def join(model_state, planar_state, sagittal_state, gradient, pieces, planar_image, sagittal_image):
@@ -400,7 +409,7 @@
         tiled = values.reshape(views, agents, own, bins // LANES, LANES).transpose(0, 1, 3, 2, 4)
         return lax.dynamic_index_in_dim(tiled.reshape(spread, per, own, LANES), spot, 0, keepdims=False)
 
-    def gathered(sent):
+    def gathered(sent, sinogram, bin_weight):
         got = lax.all_to_all(sent.reshape(spread, per, own, LANES), PLANE, 0, 0)
         half = got.astype(f32).sum(axis=0)
         other = lax.ppermute(half, "zh", [(0, 1), (1, 0)])
@@ -408,24 +417,32 @@
         misfit = lax.all_to_all(spreaded, PLANE, 0, 0)
         return misfit.reshape(spread * per, own, LANES)
 
-    low = model_state.astype(bf16)
-    parts = [low] + [swap(low, agents, k) for k in range(1, agents)]
-    chip = mask_blocks(view_tile, block_mask)
-    sent, anchor, matrix = project_first(parts, chip, agent)
+    parts = [model_state] + [swap(model_state, agents, k) for k in range(1, agents)]
+    kept, rest = mask_blocks(view_tile, block_mask.transpose(0, 2, 1, 3))
+    sent, anchor, main = project_first(parts, kept, rest, agent)
 
     edge = HALO * LANES
-    sent, plane, side, tile_at = lax.optimization_barrier((sent, planar_state, sagittal_state, tile_at))
-    plane_low = lax.ppermute(plane[:, -edge:], TILE, line(tiles, 1))
-    plane_high = lax.ppermute(plane[:, :edge], TILE, line(tiles, -1))
+    sent, plane, side, tile_at, sinogram, bin_weight = lax.optimization_barrier(
+        (sent, planar_state, sagittal_state, tile_at, sinogram, bin_weight)
+    )
+    begin, end = plane[:, :edge], plane[:, -edge:]
+    ends = spot == spread - 1
+    across = swap(jnp.where(ends, end, begin), 2, 1, "zh")
+    upper = lax.axis_index("zh") == 1
+    blank = jnp.zeros_like(begin)
+    up = jnp.where(ends, jnp.where(upper, across, blank), end)
+    down = jnp.where(spot == 0, jnp.where(upper, blank, across), begin)
+    plane_low = lax.ppermute(up, PLANE, [(i, (i + 1) % spread) for i in range(spread)])
+    plane_high = lax.ppermute(down, PLANE, [((i + 1) % spread, i) for i in range(spread)])
     side_low = lax.ppermute(side[-HALO:], "agent", line(agents, 1))
     side_high = lax.ppermute(side[:HALO], "agent", line(agents, -1))
 
-    misfit = gathered(sent)
-    total, piece, chip = back_project(misfit, matrix, agent, agents, True)
+    misfit = gathered(sent, sinogram, bin_weight)
+    total, piece, rest = back_project(misfit, kept, main, agent, agents, True)
     pieces = [total] + [swap(piece, agents, k) for k in range(1, agents)]
-    sent, gradient = project_next(anchor, pieces, chip, agent)
-    misfit = gathered(sent)
-    pieces = back_project(misfit, matrix, agent, agents, False)
+    sent, gradient = project_next(anchor, pieces, kept, rest, agent)
+    misfit = gathered(sent, sinogram, bin_weight)
+    pieces = back_project(misfit, kept, main, agent, agents, False)
     pieces = [pieces[0]] + [swap(pieces[k], agents, k) for k in range(1, agents)]
     kernels = (planar_in, planar_mid, planar_out)
     planar_image = denoise(plane_low, planar_state, plane_high, *kernels, tile_at, tiles, True)

time: 122 us -> 123 us (level); the launches traced: 121 us -> 121 us
  blocking collectives: 23.6 us -> 11.8 us
  waiting for transfers between devices: 13.8 us -> 19.6 us
  starting transfers between devices: 51.6 us -> 56.9 us
  local copies, waits for them, and re-layouts: 6.89 us -> 8.75 us
    all_to_all x1 -> x0, blocking collectives: 11.7 us -> none  [gathered(): got = lax.all_to_all(sent.reshape(spread, per, own, LANES), PLANE, 0, 0)]
    all_to_all x1 -> x2, starting transfers between devices: 7.63 us -> 12.8 us  [gathered(): got = lax.all_to_all(sent.reshape(spread, per, own, LANES), PLANE, 0, 0)]
    all_to_all x1, waiting for transfers between devices: 0.01 us -> 3.05 us  [gathered(): misfit = lax.all_to_all(spreaded, PLANE, 0, 0)]
    all_to_all x1 -> x2, waiting for transfers between devices: 7.13 us -> 9.62 us  [gathered(): got = lax.all_to_all(sent.reshape(spread, per, own, LANES), PLANE, 0, 0)]
    unnamed x23 -> x26, local copies, waits for them, and re-layouts: 6.15 us -> 8.02 us
    ppermute x11 -> x12, starting transfers between devices: 22 us -> 23.6 us  [the longest x10 19.5 us: swap(): return lax.ppermute(value, axis, [(i, i ^ k) for i in range(count)])]
    ppermute x1, starting transfers between devices: 4.55 us -> 3.16 us  [body(): side_low = lax.ppermute(side[-HALO:], 'agent', line(agents, 1))]
    ppermute x11 -> x12, waiting for transfers between devices: 5.74 us -> 5.94 us  [the longest x10 5.92 us: swap(): return lax.ppermute(value, axis, [(i, i ^ k) for i in range(count)])]
  transfers between devices with their start and end apart: 17 -> 19, of which waited for: 4 -> 7; matrix products, arithmetic and copies ran while one was open for 1% -> 1% of each run, Pallas kernels for 12% -> 11%
where the time goes in v2:
time: 123 us; the launch traced here: 121 us
  starting transfers between devices  56.9 us (46%)
  Pallas kernels  22.6 us (18%)
  waiting for transfers between devices  19.6 us (16%)
  blocking collectives  11.8 us (10%)
  local copies, waits for them, and re-layouts  8.75 us (7%)
    ppermute x10, starting transfers between devices, swap(): return lax.ppermute(value, axis, [(i, i ^ k) for i in range(count)])  19.5 us
    all_to_all x2, starting transfers between devices, gathered(): got = lax.all_to_all(sent.reshape(spread, per, own, LANES), PLANE, 0, 0)  12.8 us
    all_to_all x1, blocking collectives, gathered(): misfit = lax.all_to_all(spreaded, PLANE, 0, 0)  11.8 us
    ppermute x2, starting transfers between devices, gathered(): other = lax.ppermute(half, 'zh', [(0, 1), (1, 0)])  10.9 us
    all_to_all x2, waiting for transfers between devices, gathered(): got = lax.all_to_all(sent.reshape(spread, per, own, LANES), PLANE, 0, 0)  9.62 us
    unnamed x26, local copies, waits for them, and re-layouts  8.02 us
    pallas_call x2, Pallas kernels, denoise(): pl.pallas_call(kernel, out_shape=jax.ShapeDtypeStruct((rows, width), f32)...  6.68 us
    ppermute x10, waiting for transfers between devices, swap(): return lax.ppermute(value, axis, [(i, i ^ k) for i in range(count)])  5.92 us
  transfers between devices with their start and end apart: 19, of which 7 were waited for; matrix products, arithmetic and copies ran while one was open for 1% of the time, Pallas kernels for 11%

profile of v2, /device:TPU:2, one launch (start us, length us, event | category | flops | bytes accessed | tf_op | source)
XLA Modules:
  0.0 120.6 jit_solution(7272089768491217281)
XLA Ops:
  0.6 0.0 copy-start.8
  0.6 2.0 %collective-permute-start = (f32[8,1024]{1,0:T(8,128)}, f32[8,1024]{1,0:T(8,128)S(1)}, u32[]{:S(2)}, u32[]{:S(2)}) collective-permute-start(f32[8,1024]{1,0:T(8,128)} %bitcast.33), channel_id=1, source_target_pairs={{0,1},{1,0},{2,3},{3,2},{4,5},{5,4},{6,7},{7,6},{8,9},{9,8},{10,11... | collective-permute-start | bytes 98312 | tf_op jit(solution)/shard_map/ppermute | solution.py:349
  2.6 3.3 %collective-permute-start.1 = (f32[8,1024]{1,0:T(8,128)}, f32[8,1024]{1,0:T(8,128)S(1)}, u32[]{:S(2)}, u32[]{:S(2)}) collective-permute-start(f32[8,1024]{1,0:T(8,128)} %bitcast.34), channel_id=1, source_target_pairs={{0,2},{1,3},{2,0},{3,1},{4,6},{5,7},{6,4},{7,5},{8,10},{9,11},{10,... | collective-permute-start | bytes 98312 | tf_op jit(solution)/shard_map/ppermute | solution.py:349
  5.9 0.0 collective-permute-start.2
  5.9 3.8 %mask_blocks.1 = (bf16[3,384,1024]{2,1,0:T(8,128)(2,1)S(1)}, bf16[5,384,1024]{2,1,0:T(8,128)(2,1)S(1)}) custom-call(s32[4,6,1,8]{3,2,1,0:T(1,128)} %bitcast.38, bf16[4,1,768,1024]{3,2,1,0:T(8,128)(2,1)} %view_ref.1), custom_call_target="tpu_custom_call" | custom-call | tf_op jit(solution)/shard_map/mask_blocks/pallas_call | solution.py:70
  9.7 0.0 copy-start
  9.8 1.9 %copy-done = bf16[5,384,1024]{2,1,0:T(8,128)(2,1)} copy-done((bf16[5,384,1024]{2,1,0:T(8,128)(2,1)}, bf16[5,384,1024]{2,1,0:T(8,128)(2,1)S(1)}, u32[]{:S(2)}) %copy-start) | copy-done | bytes 3932184
  11.6 0.0 collective-permute-done.refs_1_
  11.6 0.0 collective-permute-done.1.refs_2_
  11.6 0.2 collective-permute-done.2.refs_3_
  11.8 0.0 copy-done.8
  11.8 2.1 %copy-done.1 = bf16[5,384,1024]{2,1,0:T(8,128)(2,1)S(1)} copy-done((bf16[5,384,1024]{2,1,0:T(8,128)(2,1)S(1)}, bf16[5,384,1024]{2,1,0:T(8,128)(2,1)}, u32[]{:S(2)}) %copy-start.1) | copy-done | bytes 3932184
  14.0 3.3 %project_first.1 = (bf16[96,8,128]{2,1,0:T(8,128)(2,1)}, f32[32,1024]{1,0:T(8,128)S(1)}, bf16[5,384,1024]{2,1,0:T(8,128)(2,1)}) custom-call(s32[1]{0:T(128)} %bitcast.3.me_ref.at_ref, f32[8,1024]{1,0:T(8,128)S(1)} %bitcast.36, f32[8,1024]{1,0:T(8,128)S(1)} %collective-permute-done.refs_1_, f32[8,1024]{1,0:T(8,128)S(1)} %collective-permute-done.1.refs_2_, ...), custom_call_target="tpu_custom_call" | custom-call | tf_op jit(solution)/shard_map/project_first/pallas_call | solution.py:113
  17.3 7.6 %all-to-all-start = ((bf16[32,3,8,128]{3,2,1,0:T(8,128)(2,1)}), bf16[32,3,8,128]{3,2,1,0:T(8,128)(2,1)S(1)}, u32[]{:S(2)}, u32[]{:S(2)}) async-start(bf16[32,3,8,128]{3,2,1,0:T(8,128)(2,1)} %bitcast.6), calls=%async_computation | async-start | bytes 393216 | tf_op jit(solution)/shard_map/all_to_all | solution.py:413
  24.9 7.1 %all-to-all-done = bf16[32,3,8,128]{3,2,1,0:T(8,128)(2,1)S(1)} async-done(((bf16[32,3,8,128]{3,2,1,0:T(8,128)(2,1)}), bf16[32,3,8,128]{3,2,1,0:T(8,128)(2,1)S(1)}, u32[]{:S(2)}, u32[]{:S(2)}) %all-to-all-start) | async-done | bytes 196640 | tf_op jit(solution)/shard_map/all_to_all | solution.py:413
  32.1 6.3 %collective-permute-start.3 = (f32[3,8,128]{2,1,0:T(8,128)S(1)}, f32[3,8,128]{2,1,0:T(8,128)S(1)}, u32[]{:S(2)}, u32[]{:S(2)}) collective-permute-start(f32[3,8,128]{2,1,0:T(8,128)S(1)} %convert_reduce_fusion.1.half_ref), channel_id=1, source_target_pairs={{0,128},{128,0},{1,129},{129,1},{2,130},{130,2},{3,131},{131,3},{4... | collective-permute-start | bytes 36872 | tf_op jit(solution)/shard_map/ppermute | solution.py:415
  38.4 0.7 dynamic-slice_bitcast_fusion
  39.1 0.9 collective-permute-done.3.other_ref
  40.1 11.8 %all_to_all.20 = bf16[32,3,8,128]{3,2,1,0:T(8,128)(2,1)S(1)} all-to-all(bf16[32,3,8,128]{3,2,1,0:T(8,128)(2,1)S(1)} %spread_misfit.2), channel_id=1, replica_groups=mesh['zh'=2,'x'=4,'y'=4,'core'=2,'agent'=4] {'x','y','core'}, dimensions={0} | all-to-all | bytes 393216 | tf_op jit(solution)/shard_map/all_to_all | solution.py:417
  51.9 2.4 %back_project.2 = (f32[32,1024]{1,0:T(8,128)S(1)}, bf16[32,1024]{1,0:T(8,128)(2,1)S(1)}, bf16[5,384,1024]{2,1,0:T(8,128)(2,1)S(1)}) custom-call(s32[1]{0:T(128)} %bitcast.3.me_ref.at_ref, bf16[96,8,128]{2,1,0:T(8,128)(2,1)S(1)} %bitcast.25, bf16[3,384,1024]{2,1,0:T(8,128)(2,1)S(1)} %get-tuple-element.23.refs_4_.kept_ref, ...), custom_call_target="tpu_custom_call" | custom-call | tf_op jit(solution)/shard_map/back_project/pallas_call | solution.py:202
  54.3 0.0 copy-start.2
  54.3 1.9 %copy-done.2 = bf16[5,384,1024]{2,1,0:T(8,128)(2,1)} copy-done((bf16[5,384,1024]{2,1,0:T(8,128)(2,1)}, bf16[5,384,1024]{2,1,0:T(8,128)(2,1)S(1)}, u32[]{:S(2)}) %copy-start.2) | copy-done | bytes 3932184
  56.2 0.1 collective-permute-start.4
  56.4 3.8 %collective-permute-start.5 = (bf16[32,1024]{1,0:T(8,128)(2,1)S(1)}, bf16[32,1024]{1,0:T(8,128)(2,1)S(1)}, u32[]{:S(2)}, u32[]{:S(2)}) collective-permute-start(bf16[32,1024]{1,0:T(8,128)(2,1)S(1)} %get-tuple-element.32), channel_id=1, source_target_pairs={{0,2},{1,3},{2,0},{3,1},{4,6},{5,7},{6,4},{7,5},{8,10},{9,11},{10,... | collective-permute-start | bytes 196616 | tf_op jit(solution)/shard_map/ppermute | solution.py:349
  60.1 0.5 collective-permute-start.6
  60.6 0.0 collective-permute-done.4.refs_1_
  60.6 3.6 %collective-permute-done.5.refs_2_ = bf16[32,1024]{1,0:T(8,128)(2,1)S(1)} collective-permute-done((bf16[32,1024]{1,0:T(8,128)(2,1)S(1)}, bf16[32,1024]{1,0:T(8,128)(2,1)S(1)}, u32[]{:S(2)}, u32[]{:S(2)}) %collective-permute-start.5) | collective-permute-done | bytes 65568 | tf_op jit(solution)/shard_map/ppermute | solution.py:349
  64.2 2.1 %collective-permute-done.6.refs_3_ = bf16[32,1024]{1,0:T(8,128)(2,1)S(1)} collective-permute-done((bf16[32,1024]{1,0:T(8,128)(2,1)S(1)}, bf16[32,1024]{1,0:T(8,128)(2,1)S(1)}, u32[]{:S(2)}, u32[]{:S(2)}) %collective-permute-start.6) | collective-permute-done | bytes 65568 | tf_op jit(solution)/shard_map/ppermute | solution.py:349
  66.3 2.1 %copy-done.3 = bf16[5,384,1024]{2,1,0:T(8,128)(2,1)S(1)} copy-done((bf16[5,384,1024]{2,1,0:T(8,128)(2,1)S(1)}, bf16[5,384,1024]{2,1,0:T(8,128)(2,1)}, u32[]{:S(2)}) %copy-start.3) | copy-done | bytes 3932184
  68.4 2.6 %project_next.1 = (bf16[96,8,128]{2,1,0:T(8,128)(2,1)}, f32[8,1024]{1,0:T(8,128)S(1)}) custom-call(s32[1]{0:T(128)} %bitcast.3.me_ref.at_ref, f32[32,1024]{1,0:T(8,128)S(1)} %get-tuple-element.25.anchor_ref, f32[32,1024]{1,0:T(8,128)S(1)} %get-tuple-element.31.refs_0_, bf16[32,1024]{1,0:T(8,128)(2,1)S(1)} %collective-permute-done.4.refs_1_, ...), custom_call_target="tpu_custom_call" | custom-call | tf_op jit(solution)/shard_map/project_next/pallas_call | solution.py:144
  71.0 5.2 %all-to-all-start.2 = ((bf16[32,3,8,128]{3,2,1,0:T(8,128)(2,1)}), bf16[32,3,8,128]{3,2,1,0:T(8,128)(2,1)S(1)}, u32[]{:S(2)}, u32[]{:S(2)}) async-start(bf16[32,3,8,128]{3,2,1,0:T(8,128)(2,1)} %bitcast.16), calls=%async_computation.2 | async-start | bytes 393216 | tf_op jit(solution)/shard_map/all_to_all | solution.py:413
  76.2 0.0 copy-done.4
  76.2 0.0 copy-start.7
  76.3 0.0 copy-start.11
  76.3 0.0 copy-start.12
  76.3 4.7 %collective-permute-start.7 = (f32[8,640]{1,0:T(8,128)S(1)}, f32[8,640]{1,0:T(8,128)S(1)}, u32[]{:S(2)}, u32[]{:S(2)}) collective-permute-start(f32[8,640]{1,0:T(8,128)S(1)} %slice_select_fusion), channel_id=1, source_target_pairs={{0,128},{128,0},{1,129},{129,1},{2,130},{130,2},{3,131},{131,3},{4... | collective-permute-start | bytes 61448 | tf_op jit(solution)/shard_map/ppermute | solution.py:349
  80.9 2.5 %all-to-all-done.2 = bf16[32,3,8,128]{3,2,1,0:T(8,128)(2,1)S(1)} async-done(((bf16[32,3,8,128]{3,2,1,0:T(8,128)(2,1)}), bf16[32,3,8,128]{3,2,1,0:T(8,128)(2,1)S(1)}, u32[]{:S(2)}, u32[]{:S(2)}) %all-to-all-start.2) | async-done | bytes 196640 | tf_op jit(solution)/shard_map/all_to_all | solution.py:413
  83.5 4.7 %collective-permute-start.12 = (f32[3,8,128]{2,1,0:T(8,128)S(1)}, f32[3,8,128]{2,1,0:T(8,128)S(1)}, u32[]{:S(2)}, u32[]{:S(2)}) collective-permute-start(f32[3,8,128]{2,1,0:T(8,128)S(1)} %convert_reduce_fusion.half_ref), channel_id=1, source_target_pairs={{0,128},{128,0},{1,129},{129,1},{2,130},{130,2},{3,131},{131,3},{4... | collective-permute-start | bytes 36872 | tf_op jit(solution)/shard_map/ppermute | solution.py:415
  88.1 3.2 %collective-permute-start.10 = (f32[5,1024]{1,0:T(8,128)S(1)}, f32[5,1024]{1,0:T(8,128)S(1)}, u32[]{:S(2)}, u32[]{:S(2)}) collective-permute-start(f32[5,1024]{1,0:T(8,128)S(1)} %get-tuple-element.46), channel_id=1, source_target_pairs={{0,1},{1,2},{2,3},{4,5},{5,6},{6,7},{8,9},{9,10},{10,11},{12,13},{... | collective-permute-start | bytes 61448 | tf_op jit(solution)/shard_map/ppermute | solution.py:437
  91.3 1.3 %collective-permute-start.11 = (f32[5,1024]{1,0:T(8,128)S(1)}, f32[5,1024]{1,0:T(8,128)S(1)}, u32[]{:S(2)}, u32[]{:S(2)}) collective-permute-start(f32[5,1024]{1,0:T(8,128)S(1)} %get-tuple-element.45), channel_id=1, source_target_pairs={{1,0},{2,1},{3,2},{5,4},{6,5},{7,6},{9,8},{10,9},{11,10},{13,12},{... | collective-permute-start | bytes 61448 | tf_op jit(solution)/shard_map/ppermute | solution.py:438
  92.6 0.0 collective-permute-done.12.other_ref
  92.6 0.7 spread_misfit.3
  93.3 5.0 %all-to-all-start.3 = ((bf16[32,3,8,128]{3,2,1,0:T(8,128)(2,1)}), bf16[32,3,8,128]{3,2,1,0:T(8,128)(2,1)S(1)}, u32[]{:S(2)}, u32[]{:S(2)}) async-start(bf16[32,3,8,128]{3,2,1,0:T(8,128)(2,1)} %spread_misfit.3), calls=%async_computation.3 | async-start | bytes 393216 | tf_op jit(solution)/shard_map/all_to_all | solution.py:417
  98.3 0.0 collective-permute-done.7
  98.4 0.4 collective-permute-start.8
  98.8 3.7 %collective-permute-start.9 = (f32[8,640]{1,0:T(8,128)S(1)}, f32[8,640]{1,0:T(8,128)S(1)}, u32[]{:S(2)}, u32[]{:S(2)}) collective-permute-start(f32[8,640]{1,0:T(8,128)S(1)} %get-tuple-element.43), channel_id=1, source_target_pairs={{4,0},{8,4},{12,8},{16,12},{20,16},{24,20},{28,24},{32,28},{36,32}... | collective-permute-start | bytes 61448 | tf_op jit(solution)/shard_map/ppermute | solution.py:436
  102.5 3.1 %all-to-all-done.3 = bf16[32,3,8,128]{3,2,1,0:T(8,128)(2,1)S(1)} async-done(((bf16[32,3,8,128]{3,2,1,0:T(8,128)(2,1)}), bf16[32,3,8,128]{3,2,1,0:T(8,128)(2,1)S(1)}, u32[]{:S(2)}, u32[]{:S(2)}) %all-to-all-start.3) | async-done | bytes 196640 | tf_op jit(solution)/shard_map/all_to_all | solution.py:417
  105.5 2.4 %back_project.3 = (f32[8,1024]{1,0:T(8,128)S(1)}, bf16[8,1024]{1,0:T(8,128)(2,1)S(1)}, bf16[8,1024]{1,0:T(8,128)(2,1)S(1)}, bf16[8,1024]{1,0:T(8,128)(2,1)S(1)}) custom-call(s32[1]{0:T(128)} %bitcast.3.me_ref.at_ref, bf16[96,8,128]{2,1,0:T(8,128)(2,1)S(1)} %bitcast.24, bf16[3,384,1024]{2,1,0:T(8,128)(2,1)S(1)} %get-tuple-element.23.refs_4_.kept_ref, ...), custom_call_target="tpu_custom_call" | custom-call | tf_op jit(solution)/shard_map/back_project/pallas_call | solution.py:202
  107.9 2.7 %collective-permute-start.13 = (bf16[8,1024]{1,0:T(8,128)(2,1)S(1)}, bf16[8,1024]{1,0:T(8,128)(2,1)S(1)}, u32[]{:S(2)}, u32[]{:S(2)}) collective-permute-start(bf16[8,1024]{1,0:T(8,128)(2,1)S(1)} %get-tuple-element.40), channel_id=1, source_target_pairs={{0,1},{1,0},{2,3},{3,2},{4,5},{5,4},{6,7},{7,6},{8,9},{9,8},{10,11... | collective-permute-start | bytes 49160 | tf_op jit(solution)/shard_map/ppermute | solution.py:349
  110.7 0.0 collective-permute-done.10.low_ref
  110.7 1.2 collective-permute-start.14
  111.9 0.0 collective-permute-done.11.high_ref
  111.9 1.3 %collective-permute-start.15 = (bf16[8,1024]{1,0:T(8,128)(2,1)S(1)}, bf16[8,1024]{1,0:T(8,128)(2,1)S(1)}, u32[]{:S(2)}, u32[]{:S(2)}) collective-permute-start(bf16[8,1024]{1,0:T(8,128)(2,1)S(1)} %get-tuple-element.42), channel_id=1, source_target_pairs={{0,3},{1,2},{2,1},{3,0},{4,7},{5,6},{6,5},{7,4},{8,11},{9,10},{10,... | collective-permute-start | bytes 49160 | tf_op jit(solution)/shard_map/ppermute | solution.py:349
  113.2 3.3 %denoise.3.refs_5_ = f32[8,1024]{1,0:T(8,128)S(1)} custom-call(s32[1]{0:T(128)} %bitcast.3.me_ref.at_ref, f32[5,1024]{1,0:T(8,128)S(1)} %collective-permute-done.10.low_ref, f32[8,1024]{1,0:T(8,128)S(1)} %bitcast.31, f32[5,1024]{1,0:T(8,128)S(1)} %collective-permute-done.11.high_ref, f32[9,16]{1,0:T(8,128)S(1)} %copy-done.9, f32[3,9,16,16]{3,2,1,0:T(8,128)S(1)} %copy-done.6, ...), custom_call_target="tpu_custom_call" | custom-call | tf_op jit(solution)/shard_map/denoise/pallas_call | solution.py:333
  116.5 0.0 collective-permute-done.8.low_ref
  116.5 0.0 collective-permute-done.9.high_ref
  116.5 0.0 copy-done.7
  116.5 0.0 copy-done.11
  116.5 0.0 copy-done.12
  116.5 3.4 %denoise.2.refs_4_ = f32[8,1024]{1,0:T(8,128)S(1)} custom-call(s32[1]{0:T(128)} %bitcast.5.at_ref, f32[8,640]{1,0:T(8,128)S(1)} %collective-permute-done.8.low_ref, f32[8,1024]{1,0:T(8,128)S(1)} %bitcast.28, f32[8,640]{1,0:T(8,128)S(1)} %collective-permute-done.9.high_ref, f32[9,16]{1,0:T(8,128)S(1)} %copy-done.11, f32[3,9,16,16]{3,2,1,0:T(8,128)S(1)} %copy-done.7, ...), custom_call_target="tpu_custom_call" | custom-call | tf_op jit(solution)/shard_map/denoise/pallas_call | solution.py:333
  119.9 0.0 collective-permute-done.13.refs_7_
  119.9 0.0 collective-permute-done.14.refs_8_
  119.9 0.0 collective-permute-done.15.refs_9_
  119.9 0.7 join.1
  (17 shorter events, 0.1 us)
Async XLA Ops:
  0.6 11.2 %copy-start.8 = (f32[1,8,1024]{2,1,0:T(8,128)S(1)}, f32[1,8,1024]{2,1,0:T(8,128)}, u32[]{:S(2)}) copy-start(f32[1,8,1024]{2,1,0:T(8,128)} %param.17) | copy-start | bytes 98308
  0.6 11.0 %collective-permute-start = (f32[8,1024]{1,0:T(8,128)}, f32[8,1024]{1,0:T(8,128)S(1)}, u32[]{:S(2)}, u32[]{:S(2)}) collective-permute-start(f32[8,1024]{1,0:T(8,128)} %bitcast.33), channel_id=1, source_target_pairs={{0,1},{1,0},{2,3},{3,2},{4,5},{5,4},{6,7},{7,6},{8,9},{9,8},{10,11... | collective-permute-start | bytes 98312 | tf_op jit(solution)/shard_map/ppermute | solution.py:349
  2.6 9.0 %collective-permute-start.1 = (f32[8,1024]{1,0:T(8,128)}, f32[8,1024]{1,0:T(8,128)S(1)}, u32[]{:S(2)}, u32[]{:S(2)}) collective-permute-start(f32[8,1024]{1,0:T(8,128)} %bitcast.34), channel_id=1, source_target_pairs={{0,2},{1,3},{2,0},{3,1},{4,6},{5,7},{6,4},{7,5},{8,10},{9,11},{10,... | collective-permute-start | bytes 98312 | tf_op jit(solution)/shard_map/ppermute | solution.py:349
  5.9 5.9 %collective-permute-start.2 = (f32[8,1024]{1,0:T(8,128)}, f32[8,1024]{1,0:T(8,128)S(1)}, u32[]{:S(2)}, u32[]{:S(2)}) collective-permute-start(f32[8,1024]{1,0:T(8,128)} %bitcast.35), channel_id=1, source_target_pairs={{0,3},{1,2},{2,1},{3,0},{4,7},{5,6},{6,5},{7,4},{8,11},{9,10},{10,... | collective-permute-start | bytes 98312 | tf_op jit(solution)/shard_map/ppermute | solution.py:349
  9.7 1.9 %copy-start = (bf16[5,384,1024]{2,1,0:T(8,128)(2,1)}, bf16[5,384,1024]{2,1,0:T(8,128)(2,1)S(1)}, u32[]{:S(2)}) copy-start(bf16[5,384,1024]{2,1,0:T(8,128)(2,1)S(1)} %get-tuple-element.24.refs_5_) | copy-start | bytes 11796484
  11.8 2.1 %copy-start.1 = (bf16[5,384,1024]{2,1,0:T(8,128)(2,1)S(1)}, bf16[5,384,1024]{2,1,0:T(8,128)(2,1)}, u32[]{:S(2)}) copy-start(bf16[5,384,1024]{2,1,0:T(8,128)(2,1)} %copy-done) | copy-start | bytes 11796484
  17.3 14.8 %all-to-all-start = ((bf16[32,3,8,128]{3,2,1,0:T(8,128)(2,1)}), bf16[32,3,8,128]{3,2,1,0:T(8,128)(2,1)S(1)}, u32[]{:S(2)}, u32[]{:S(2)}) async-start(bf16[32,3,8,128]{3,2,1,0:T(8,128)(2,1)} %bitcast.6), calls=%async_computation | async-start | bytes 393216 | tf_op jit(solution)/shard_map/all_to_all | solution.py:413
  32.1 8.0 %collective-permute-start.3 = (f32[3,8,128]{2,1,0:T(8,128)S(1)}, f32[3,8,128]{2,1,0:T(8,128)S(1)}, u32[]{:S(2)}, u32[]{:S(2)}) collective-permute-start(f32[3,8,128]{2,1,0:T(8,128)S(1)} %convert_reduce_fusion.1.half_ref), channel_id=1, source_target_pairs={{0,128},{128,0},{1,129},{129,1},{2,130},{130,2},{3,131},{131,3},{4... | collective-permute-start | bytes 36872 | tf_op jit(solution)/shard_map/ppermute | solution.py:415
  51.9 24.3 %copy-start.4 = (f32[1,8,1024]{2,1,0:T(8,128)S(1)}, f32[1,8,1024]{2,1,0:T(8,128)}, u32[]{:S(2)}) copy-start(f32[1,8,1024]{2,1,0:T(8,128)} %param.18) | copy-start | bytes 98308
  51.9 36.2 %copy-start.5 = (f32[1,8,1024]{2,1,0:T(8,128)S(1)}, f32[1,8,1024]{2,1,0:T(8,128)}, u32[]{:S(2)}) copy-start(f32[1,8,1024]{2,1,0:T(8,128)} %param.19) | copy-start | bytes 98308
  54.3 1.9 %copy-start.2 = (bf16[5,384,1024]{2,1,0:T(8,128)(2,1)}, bf16[5,384,1024]{2,1,0:T(8,128)(2,1)S(1)}, u32[]{:S(2)}) copy-start(bf16[5,384,1024]{2,1,0:T(8,128)(2,1)S(1)} %get-tuple-element.33.refs_5_) | copy-start | bytes 11796484
  56.2 4.4 %collective-permute-start.4 = (bf16[32,1024]{1,0:T(8,128)(2,1)S(1)}, bf16[32,1024]{1,0:T(8,128)(2,1)S(1)}, u32[]{:S(2)}, u32[]{:S(2)}) collective-permute-start(bf16[32,1024]{1,0:T(8,128)(2,1)S(1)} %get-tuple-element.32), channel_id=1, source_target_pairs={{0,1},{1,0},{2,3},{3,2},{4,5},{5,4},{6,7},{7,6},{8,9},{9,8},{10,11... | collective-permute-start | bytes 196616 | tf_op jit(solution)/shard_map/ppermute | solution.py:349
  56.4 7.9 %collective-permute-start.5 = (bf16[32,1024]{1,0:T(8,128)(2,1)S(1)}, bf16[32,1024]{1,0:T(8,128)(2,1)S(1)}, u32[]{:S(2)}, u32[]{:S(2)}) collective-permute-start(bf16[32,1024]{1,0:T(8,128)(2,1)S(1)} %get-tuple-element.32), channel_id=1, source_target_pairs={{0,2},{1,3},{2,0},{3,1},{4,6},{5,7},{6,4},{7,5},{8,10},{9,11},{10,... | collective-permute-start | bytes 196616 | tf_op jit(solution)/shard_map/ppermute | solution.py:349
  60.1 6.2 %collective-permute-start.6 = (bf16[32,1024]{1,0:T(8,128)(2,1)S(1)}, bf16[32,1024]{1,0:T(8,128)(2,1)S(1)}, u32[]{:S(2)}, u32[]{:S(2)}) collective-permute-start(bf16[32,1024]{1,0:T(8,128)(2,1)S(1)} %get-tuple-element.32), channel_id=1, source_target_pairs={{0,3},{1,2},{2,1},{3,0},{4,7},{5,6},{6,5},{7,4},{8,11},{9,10},{10,... | collective-permute-start | bytes 196616 | tf_op jit(solution)/shard_map/ppermute | solution.py:349
  66.3 2.1 %copy-start.3 = (bf16[5,384,1024]{2,1,0:T(8,128)(2,1)S(1)}, bf16[5,384,1024]{2,1,0:T(8,128)(2,1)}, u32[]{:S(2)}) copy-start(bf16[5,384,1024]{2,1,0:T(8,128)(2,1)} %copy-done.2) | copy-start | bytes 11796484
  71.0 42.1 %copy-start.6 = (f32[3,9,16,16]{3,2,1,0:T(8,128)S(1)}, f32[3,9,16,16]{3,2,1,0:T(8,128)}, u32[]{:S(2)}) copy-start(f32[3,9,16,16]{3,2,1,0:T(8,128)} %mid_ref.3) | copy-start | bytes 82948
  71.0 42.1 %copy-start.9 = (f32[9,16]{1,0:T(8,128)S(1)}, f32[9,16]{1,0:T(8,128)}, u32[]{:S(2)}) copy-start(f32[9,16]{1,0:T(8,128)} %first_ref.3) | copy-start | bytes 1732
  71.0 42.1 %copy-start.10 = (f32[9,16]{1,0:T(8,128)S(1)}, f32[9,16]{1,0:T(8,128)}, u32[]{:S(2)}) copy-start(f32[9,16]{1,0:T(8,128)} %last_ref.3) | copy-start | bytes 1732
  71.0 12.4 %all-to-all-start.2 = ((bf16[32,3,8,128]{3,2,1,0:T(8,128)(2,1)}), bf16[32,3,8,128]{3,2,1,0:T(8,128)(2,1)S(1)}, u32[]{:S(2)}, u32[]{:S(2)}) async-start(bf16[32,3,8,128]{3,2,1,0:T(8,128)(2,1)} %bitcast.16), calls=%async_computation.2 | async-start | bytes 393216 | tf_op jit(solution)/shard_map/all_to_all | solution.py:413
  76.2 40.3 %copy-start.7 = (f32[3,9,16,16]{3,2,1,0:T(8,128)S(1)}, f32[3,9,16,16]{3,2,1,0:T(8,128)}, u32[]{:S(2)}) copy-start(f32[3,9,16,16]{3,2,1,0:T(8,128)} %mid_ref.2) | copy-start | bytes 82948
  76.3 40.3 %copy-start.11 = (f32[9,16]{1,0:T(8,128)S(1)}, f32[9,16]{1,0:T(8,128)}, u32[]{:S(2)}) copy-start(f32[9,16]{1,0:T(8,128)} %first_ref.2) | copy-start | bytes 1732
  76.3 40.3 %copy-start.12 = (f32[9,16]{1,0:T(8,128)S(1)}, f32[9,16]{1,0:T(8,128)}, u32[]{:S(2)}) copy-start(f32[9,16]{1,0:T(8,128)} %last_ref.2) | copy-start | bytes 1732
  76.3 22.1 %collective-permute-start.7 = (f32[8,640]{1,0:T(8,128)S(1)}, f32[8,640]{1,0:T(8,128)S(1)}, u32[]{:S(2)}, u32[]{:S(2)}) collective-permute-start(f32[8,640]{1,0:T(8,128)S(1)} %slice_select_fusion), channel_id=1, source_target_pairs={{0,128},{128,0},{1,129},{129,1},{2,130},{130,2},{3,131},{131,3},{4... | collective-permute-start | bytes 61448 | tf_op jit(solution)/shard_map/ppermute | solution.py:349
  83.5 9.1 %collective-permute-start.12 = (f32[3,8,128]{2,1,0:T(8,128)S(1)}, f32[3,8,128]{2,1,0:T(8,128)S(1)}, u32[]{:S(2)}, u32[]{:S(2)}) collective-permute-start(f32[3,8,128]{2,1,0:T(8,128)S(1)} %convert_reduce_fusion.half_ref), channel_id=1, source_target_pairs={{0,128},{128,0},{1,129},{129,1},{2,130},{130,2},{3,131},{131,3},{4... | collective-permute-start | bytes 36872 | tf_op jit(solution)/shard_map/ppermute | solution.py:415
  88.1 22.5 %collective-permute-start.10 = (f32[5,1024]{1,0:T(8,128)S(1)}, f32[5,1024]{1,0:T(8,128)S(1)}, u32[]{:S(2)}, u32[]{:S(2)}) collective-permute-start(f32[5,1024]{1,0:T(8,128)S(1)} %get-tuple-element.46), channel_id=1, source_target_pairs={{0,1},{1,2},{2,3},{4,5},{5,6},{6,7},{8,9},{9,10},{10,11},{12,13},{... | collective-permute-start | bytes 61448 | tf_op jit(solution)/shard_map/ppermute | solution.py:437
  91.3 20.6 %collective-permute-start.11 = (f32[5,1024]{1,0:T(8,128)S(1)}, f32[5,1024]{1,0:T(8,128)S(1)}, u32[]{:S(2)}, u32[]{:S(2)}) collective-permute-start(f32[5,1024]{1,0:T(8,128)S(1)} %get-tuple-element.45), channel_id=1, source_target_pairs={{1,0},{2,1},{3,2},{5,4},{6,5},{7,6},{9,8},{10,9},{11,10},{13,12},{... | collective-permute-start | bytes 61448 | tf_op jit(solution)/shard_map/ppermute | solution.py:438
  93.3 12.2 %all-to-all-start.3 = ((bf16[32,3,8,128]{3,2,1,0:T(8,128)(2,1)}), bf16[32,3,8,128]{3,2,1,0:T(8,128)(2,1)S(1)}, u32[]{:S(2)}, u32[]{:S(2)}) async-start(bf16[32,3,8,128]{3,2,1,0:T(8,128)(2,1)} %spread_misfit.3), calls=%async_computation.3 | async-start | bytes 393216 | tf_op jit(solution)/shard_map/all_to_all | solution.py:417
  98.4 18.1 %collective-permute-start.8 = (f32[8,640]{1,0:T(8,128)S(1)}, f32[8,640]{1,0:T(8,128)S(1)}, u32[]{:S(2)}, u32[]{:S(2)}) collective-permute-start(f32[8,640]{1,0:T(8,128)S(1)} %get-tuple-element.44), channel_id=1, source_target_pairs={{0,4},{4,8},{8,12},{12,16},{16,20},{20,24},{24,28},{28,32},{32,36}... | collective-permute-start | bytes 61448 | tf_op jit(solution)/shard_map/ppermute | solution.py:435
  98.8 17.7 %collective-permute-start.9 = (f32[8,640]{1,0:T(8,128)S(1)}, f32[8,640]{1,0:T(8,128)S(1)}, u32[]{:S(2)}, u32[]{:S(2)}) collective-permute-start(f32[8,640]{1,0:T(8,128)S(1)} %get-tuple-element.43), channel_id=1, source_target_pairs={{4,0},{8,4},{12,8},{16,12},{20,16},{24,20},{28,24},{32,28},{36,32}... | collective-permute-start | bytes 61448 | tf_op jit(solution)/shard_map/ppermute | solution.py:436
  107.9 12.0 %collective-permute-start.13 = (bf16[8,1024]{1,0:T(8,128)(2,1)S(1)}, bf16[8,1024]{1,0:T(8,128)(2,1)S(1)}, u32[]{:S(2)}, u32[]{:S(2)}) collective-permute-start(bf16[8,1024]{1,0:T(8,128)(2,1)S(1)} %get-tuple-element.40), channel_id=1, source_target_pairs={{0,1},{1,0},{2,3},{3,2},{4,5},{5,4},{6,7},{7,6},{8,9},{9,8},{10,11... | collective-permute-start | bytes 49160 | tf_op jit(solution)/shard_map/ppermute | solution.py:349
  110.7 9.2 %collective-permute-start.14 = (bf16[8,1024]{1,0:T(8,128)(2,1)S(1)}, bf16[8,1024]{1,0:T(8,128)(2,1)S(1)}, u32[]{:S(2)}, u32[]{:S(2)}) collective-permute-start(bf16[8,1024]{1,0:T(8,128)(2,1)S(1)} %get-tuple-element.41), channel_id=1, source_target_pairs={{0,2},{1,3},{2,0},{3,1},{4,6},{5,7},{6,4},{7,5},{8,10},{9,11},{10,... | collective-permute-start | bytes 49160 | tf_op jit(solution)/shard_map/ppermute | solution.py:349
  111.9 8.1 %collective-permute-start.15 = (bf16[8,1024]{1,0:T(8,128)(2,1)S(1)}, bf16[8,1024]{1,0:T(8,128)(2,1)S(1)}, u32[]{:S(2)}, u32[]{:S(2)}) collective-permute-start(bf16[8,1024]{1,0:T(8,128)(2,1)S(1)} %get-tuple-element.42), channel_id=1, source_target_pairs={{0,3},{1,2},{2,1},{3,0},{4,7},{5,6},{6,5},{7,4},{8,11},{9,10},{10,... | collective-permute-start | bytes 49160 | tf_op jit(solution)/shard_map/ppermute | solution.py:349
